TPU v7x, 32 devices: a whole 2x2x4 slice. The times are simulated.
32 devices in a mesh: win: 2 (over x), gx: 8 (over z, y), gy: 2 (over core).
Axes of the slice: x: 2, y: 2, z: 4, core: 2. Of those that a mesh axis runs over, the one named last changes fastest.
Arguments:
- mask_init: float32 [2048, 256], P(('win', 'gx'), 'gy'), parts along dimension 0, may hold values from 0 to 1
- target_map: int32 [2048, 256], P(('win', 'gx'), 'gy'), parts along dimension 0, may hold values 0 or 1
- kernels: float32 [6, 129, 129], replicated, may hold values from -0.07 to 0.07, as said below
Outputs:
- mask_out: float32 [2048, 256], P(('win', 'gx'), 'gy'), parts along dimension 0
- resist_out: float32 [2048, 256], P(('win', 'gx'), 'gy'), parts along dimension 0
There are 2 independent parts, one for each index of `win`. A program takes and returns all parts, laid end to end along the dimension named above; an argument that names none is the same for every part. Nothing has to cross between parts.
Inputs may be any that keep to these rules, and one draw needn't show every extreme that they name: Each kernel is even: kernels[k, a, b] = kernels[k, 128 - a, 128 - b].
All inputs are finite; a program needn't handle non-finite values. No bound on the sum of `target_map` on one device may be relied on, other than what follows from the above.
Results may differ from a plain program's by a relative error of at most 0.0001.
Values sent between devices are 32-bit elements; how exact they have to be, the bound alone decides.
No kernel may reach another device: no remote copies, remote signals or barrier semaphores. Data moves between devices by JAX's collectives and lax.ppermute only.
A program may use at most 64 MiB of HBM per device.

v0:
```python
import functools

import jax
import jax.numpy as jnp
import ml_dtypes
import numpy as np
from jax import lax
from jax.experimental import pallas as pl
from jax.experimental.pallas import tpu as pltpu
from jax.sharding import PartitionSpec as P

STEP = 0.1
STEEP = 4.0
THRESHOLD = 1.5
N = 256
H = 128
R = 64
VMEM = pl.BlockSpec(memory_space=pltpu.VMEM)
SMEM = pl.BlockSpec(memory_space=pltpu.SMEM)


def pair(table):
    high = table.astype(np.float32).astype(ml_dtypes.bfloat16)
    low = (table - high.astype(np.float64)).astype(np.float32).astype(ml_dtypes.bfloat16)
    return high, low


def wave_tables():
    place = np.arange(N)
    freq = np.arange(H)
    angle = 2.0 * np.pi * ((freq[:, None] * place[None, :]) % N) / N
    forward = np.concatenate([np.cos(angle), np.sin(angle)], 0)
    forward[H] = np.where(place % 2 == 0, 1.0, -1.0)
    weight = np.full((N,), 2.0)
    weight[0] = weight[H] = 1.0
    inverse = (forward * weight[:, None] / N).T
    return forward, inverse


def spectrum_tables(size, rows):
    slot = np.arange(N)
    freq = np.where(slot < H, slot, np.where(slot == H, H, slot - H))
    b = np.arange(size) - (size - 1) // 2
    right = np.zeros((N, N + H))
    right[:size, :N] = np.cos(2.0 * np.pi * ((b[:, None] * freq[None, :]) % N) / N)
    right[:size, N:] = np.sin(2.0 * np.pi * ((b[:, None] * slot[None, :H]) % N) / N)
    a = np.arange((size + 1) // 2)
    fold = np.where(a == 0, 1.0, 2.0)
    left_cos = np.zeros((N, rows))
    left_cos[:, : a.size] = fold * np.cos(2.0 * np.pi * ((freq[:, None] * a[None, :]) % N) / N)
    left_sin = np.zeros((H, rows))
    left_sin[:, : a.size] = fold * np.sin(2.0 * np.pi * ((slot[:H, None] * a[None, :]) % N) / N)
    return right, left_cos, left_sin


def split(value):
    high = value.astype(jnp.bfloat16)
    low = (value - high.astype(jnp.float32)).astype(jnp.bfloat16)
    return high, low


def dot(left, right):
    return jnp.dot(left, right, preferred_element_type=jnp.float32)


def dot3(left, right):
    return dot(left[0], right[0]) + dot(left[0], right[1]) + dot(left[1], right[0])


def mix(f, p_ref, q_ref, k):
    q = q_ref[k]
    cc, cs, sc, ss = f[:H, :H], f[:H, H:], f[H:, :H], f[H:, H:]
    return (
        p_ref[k, :H, :H] * cc + q * ss,
        p_ref[k, :H, H:] * cs - q * sc,
        p_ref[k, H:, :H] * sc - q * cs,
        p_ref[k, H:, H:] * ss + q * cc,
    )


QUADS = ((0, 0), (0, H), (H, 0), (H, H))


def amplitudes(blocks, field, p_ref, q_ref, t, f_sc, g_sc, h_sc, a_sc, core):
    ey = split(dot3(split(field), (t["ft_h"][...], t["ft_l"][...])))
    fwd = (t["f_h"][...], t["f_l"][...])
    for b in range(blocks):
        rows = slice(b * H, b * H + N)
        f_sc[b] = dot3(fwd, (ey[0][rows], ey[1][rows]))

    def body(k, carry):
        for b in range(blocks):
            parts = mix(f_sc[b], p_ref, q_ref, k)
            for (x, y), part in zip(QUADS, parts):
                high, low = split(part)
                g_sc[x : x + H, y : y + H] = high
                g_sc[N + x : N + x + H, y : y + H] = low
            out = dot(g_sc[...], t["iy"][core])
            h = out[:N, :H] + out[:N, H:] + out[N:, :H]
            high, low = split(h)
            h_sc[0, :, b * H : (b + 1) * H] = high
            h_sc[1, :, b * H : (b + 1) * H] = low
        for c in range(0, blocks, 2):
            cols = slice(c * H, c * H + N)
            both = dot(t["ix"][...], h_sc[0, :, cols])
            out = both[:H] + both[H:] + dot(t["ix"][:H], h_sc[1, :, cols])
            a_sc[k, c * H : (c + 1) * H, :] = out[:, :H]
            a_sc[k, (c + 1) * H : (c + 2) * H, :] = out[:, H:]
        return carry

    lax.fori_loop(0, p_ref.shape[0], body, 0)


def slopes(rows, count, a_sc, target, inside, w_sc):
    total = a_sc[0, :rows, :] * a_sc[0, :rows, :]
    for k in range(1, count):
        total = total + a_sc[k, :rows, :] * a_sc[k, :rows, :]
    resist = 1.0 / (1.0 + jnp.exp(-STEEP * (total - THRESHOLD)))
    slope = 2.0 * (resist - target) * STEEP * resist * (1.0 - resist)
    slope = jnp.where(inside, 2.0 * slope, 0.0)
    for k in range(count):
        high, low = split(a_sc[k, :rows, :] * slope)
        w_sc[k, :rows, :H] = high
        w_sc[k, :rows, H:] = low
    return resist


def gradients(blocks, p_ref, q_ref, t, w_sc, z_sc, core):
    rows = (blocks + 1) * H
    own = pl.ds(pl.multiple_of(core * H, H), H)
    z_sc[...] = jnp.zeros_like(z_sc)

    def body(k, carry):
        w = w_sc[k, :rows, :]
        wy = dot(w, t["fy_hh"][core]) + dot(w[:, :H], t["ft_l"][own, :])
        high, low = split(wy)
        for b in range(blocks):
            part = slice(b * H, b * H + N)
            f = dot3((t["f_h"][...], t["f_l"][...]), (high[part], low[part]))
            for (x, y), part in zip(QUADS, mix(f, p_ref, q_ref, k)):
                z_sc[b, x : x + H, y : y + H] += part
        return carry

    lax.fori_loop(0, p_ref.shape[0], body, 0)
    out = []
    for b in range(blocks):
        high, low = split(z_sc[b])
        both = dot(t["ix"][...], high)
        zx = both[:H] + both[H:] + dot(t["ix"][:H], low)
        out.append(dot3(split(zx), (t["it_h"][...], t["it_l"][...])))
    return out


def lane_mask(shape, core):
    lane = lax.broadcasted_iota(jnp.int32, shape, 1)
    return (lane >= core * R) & (lane < N - R + core * R)


def row_mask(shape, first, total):
    row = lax.broadcasted_iota(jnp.int32, shape, 0) + first
    return (row >= 0) & (row < total)


def spectrum_kernel(k_ref, rh_ref, rl_ref, ch_ref, cl_ref, sh_ref, sl_ref, p_ref, q_ref):
    count = p_ref.shape[0]
    rows = k_ref.shape[0] // count
    section = dot3(split(k_ref[...]), (rh_ref[...], rl_ref[...]))
    for k in range(count):
        high, low = split(section[k * rows : (k + 1) * rows])
        p_ref[k] = dot3((ch_ref[...], cl_ref[...]), (high[:, :N], low[:, :N]))
        q_ref[k] = dot3((sh_ref[...], sl_ref[...]), (high[:, N:], low[:, N:]))


TABLES = ("f_h", "f_l", "ft_h", "ft_l", "it_h", "it_l", "ix", "iy", "fy_hh")


def first_kernel(where_ref, own_ref, s1_ref, r1_ref, s2_ref, r2_ref, p_ref, q_ref, *refs):
    t = dict(zip(TABLES, refs))
    rest_ref, send_ref, target_ref, f_sc, g_sc, h_sc, a_sc, w_sc, z_sc = refs[len(TABLES) :]
    core, tile, total = where_ref[0], where_ref[1], where_ref[2]
    count = p_ref.shape[0]
    low1 = jnp.where(core == 0, s1_ref[...], r1_ref[...])
    upp1 = jnp.where(core == 0, r1_ref[...], s1_ref[...])
    low2 = jnp.where(core == 0, s2_ref[...], r2_ref[...])
    upp2 = jnp.where(core == 0, r2_ref[...], s2_ref[...])
    field = jnp.concatenate([low2[:H], low1[:H], own_ref[:H], upp1[:H], upp2[:H]], 0)
    inside = row_mask(field.shape, (tile - 2) * H, total) & lane_mask(field.shape, core)
    field = jnp.where(inside, field, 0.0)
    target = jnp.concatenate([low2[H:], low1[H:], own_ref[H:], upp1[H:], upp2[H:]], 0)
    target = jnp.where(core == 0, target[:, :H], target[:, H:])
    amplitudes(4, field, p_ref, q_ref, t, f_sc, g_sc, h_sc, a_sc, core)
    slopes(4 * H, count, a_sc, target, row_mask((4 * H, H), (tile - 1) * H - R, total), w_sc)
    target_ref[...] = target[H : 3 * H]
    for b, part in enumerate(gradients(3, p_ref, q_ref, t, w_sc, z_sc, core)):
        rows = slice(b * H, (b + 1) * H)
        rest_ref[rows, :] = field[(b + 1) * H : (b + 2) * H] - STEP * part
        send_ref[rows, :] = pltpu.roll(part, N - R, 1)[:, :H]


def second_kernel(where_ref, rest_ref, got_ref, target_ref, p_ref, q_ref, *refs):
    t = dict(zip(TABLES, refs))
    mask_ref, send_ref, resist_ref, f_sc, g_sc, h_sc, a_sc, w_sc, z_sc = refs[len(TABLES) :]
    core, tile, total = where_ref[0], where_ref[1], where_ref[2]
    count = p_ref.shape[0]
    got = jnp.concatenate([got_ref[...], jnp.zeros_like(got_ref)], 1)
    field = rest_ref[...] - STEP * pltpu.roll(got, R, 1)
    inside = row_mask(field.shape, (tile - 1) * H, total) & lane_mask(field.shape, core)
    field = jnp.where(inside, field, 0.0)
    amplitudes(2, field, p_ref, q_ref, t, f_sc, g_sc, h_sc, a_sc, core)
    inside = row_mask((2 * H, H), tile * H - R, total)
    resist = slopes(2 * H, count, a_sc, target_ref[...], inside, w_sc)
    resist_ref[...] = resist[R : R + H]
    (part,) = gradients(1, p_ref, q_ref, t, w_sc, z_sc, core)
    part = jnp.where(lane_mask(part.shape, core), STEP * part, 0.0)
    own = field[H : 2 * H] - part
    mask_ref[...] = jnp.where(core == 0, own[:, :H], own[:, H:])
    send_ref[...] = jnp.where(core == 0, part[:, H:], part[:, :H])


def shape(*dims, dtype=jnp.float32):
    return jax.ShapeDtypeStruct(dims, dtype)


def scratch(blocks, adjoint_blocks, count):
    return [
        pltpu.VMEM((blocks, N, N), jnp.float32),
        pltpu.VMEM((2 * N, N), jnp.bfloat16),
        pltpu.VMEM((2, N, blocks * H), jnp.bfloat16),
        pltpu.VMEM((count, blocks * H, H), jnp.float32),
        pltpu.VMEM((count, blocks * H, N), jnp.bfloat16),
        pltpu.VMEM((adjoint_blocks, N, N), jnp.float32),
    ]


def per_device(mask_init, target_map, kernels, tiles):
    count, size, _ = kernels.shape
    core = lax.axis_index("gy")
    tile = lax.axis_index("gx")
    swap = [(0, 1), (1, 0)]

    def place(step):
        step %= 2 * tiles
        return 2 * step if step < tiles else 2 * (2 * tiles - 1 - step) + 1

    def ring(shift):
        return [(place(i), place(i + shift)) for i in range(2 * tiles)]

    rows = 72
    half = jnp.pad(
        kernels[:, (size - 1) // 2 :, :],
        ((0, 0), (0, rows - (size + 1) // 2), (0, N - size)),
    ).reshape(count * rows, N)
    spectral = [jnp.asarray(v) for tab in spectrum_tables(size, rows) for v in pair(tab)]
    p, q = pl.pallas_call(
        spectrum_kernel,
        out_shape=(shape(count, N, N), shape(count, H, H)),
        in_specs=[VMEM] * 7,
        out_specs=(VMEM, VMEM),
        cost_estimate=pl.CostEstimate(
            flops=6 * count * rows * N * N * 4, bytes_accessed=4 * count * N * N, transcendentals=0
        ),
        name="spectra",
    )(half, *spectral)

    forward, inverse = wave_tables()
    f_h, f_l = pair(forward)
    i_h, i_l = pair(inverse)
    middle_h, middle_l = i_h[R : R + H], i_l[R : R + H]
    it_h, it_l = np.ascontiguousarray(i_h.T), np.ascontiguousarray(i_l.T)
    ft_h, ft_l = np.ascontiguousarray(f_h.T), np.ascontiguousarray(f_l.T)
    iy = np.stack([np.concatenate([it_h[:, c : c + H], it_l[:, c : c + H]], 1) for c in (0, H)])
    fy_hh = np.stack([np.concatenate([ft_h[c : c + H], ft_h[c : c + H]], 0) for c in (0, H)])
    ix = np.concatenate([middle_h, middle_l], 0)
    tables = [jnp.asarray(v) for v in (f_h, f_l, ft_h, ft_l, it_h, it_l, ix, iy, fy_hh)]

    mine = jnp.concatenate([mask_init, target_map.astype(jnp.float32)], 0)
    mate = lax.ppermute(mine, "gy", swap)
    own = jnp.where(
        core == 0, jnp.concatenate([mine, mate], 1), jnp.concatenate([mate, mine], 1)
    )
    far = jnp.concatenate([own[:H], jnp.where(core == 0, own[H + R :], own[H : H + R])], 0)
    s1 = lax.ppermute(own, ("gx", "gy"), ring(1))
    s2 = lax.ppermute(far, ("gx", "gy"), ring(2))
    r1 = lax.ppermute(s1, "gy", swap)
    r2 = lax.ppermute(s2, "gy", swap)

    where = jnp.stack([core, tile, jnp.int32(tiles * H)]).astype(jnp.int32)
    params = pltpu.CompilerParams(vmem_limit_bytes=56 << 20)
    rest, send, target = pl.pallas_call(
        first_kernel,
        out_shape=(shape(3 * H, N), shape(3 * H, H), shape(2 * H, H)),
        in_specs=[SMEM] + [VMEM] * (7 + len(tables)),
        out_specs=(VMEM,) * 3,
        scratch_shapes=scratch(4, 3, count),
        compiler_params=params,
        name="first_step",
    )(where, own, s1, r1, s2, r2, p, q, *tables)
    got = lax.ppermute(send, "gy", swap)
    mask, send, resist = pl.pallas_call(
        second_kernel,
        out_shape=(shape(H, H), shape(H, H), shape(H, H)),
        in_specs=[SMEM] + [VMEM] * (5 + len(tables)),
        out_specs=(VMEM,) * 3,
        scratch_shapes=scratch(2, 1, count),
        compiler_params=params,
        name="second_step",
    )(where, rest, got, target, p, q, *tables)
    return mask - lax.ppermute(send, "gy", swap), resist


def solution(mesh):
    spec = P(("win", "gx"), "gy")
    return jax.shard_map(
        functools.partial(per_device, tiles=mesh.shape["gx"]),
        mesh=mesh,
        in_specs=(spec, spec, P()),
        out_specs=(spec, spec),
        check_vma=False,
    )
```

profile of v0, /device:TPU:0, one launch (start us, length us, event | category | flops | bytes accessed | tf_op | source)
XLA Modules:
  0.0 56.7 jit_solution(10193893473550836830)
XLA Ops:
  0.6 0.0 slice-start
  0.6 0.9 %convert_element_type.5 = f32[128,128]{1,0:T(8,128)S(1)} convert(s32[128,128]{1,0:T(8,128)} %param.19) | non-fusion elementwise | flops 16384 | bytes 131072 | tf_op jit(solution)/shard_map/convert_element_type | solution.py:276
  1.5 0.8 %pad_maximum_fusion.1 = f32[256,128]{1,0:T(8,128)S(1)} fusion(f32[128,128]{1,0:T(8,128)S(1)} %convert_element_type.5, f32[128,128]{1,0:T(8,128)} %param.18), kind=kLoop, calls=%fused_computation.2 | loop fusion | flops 32768 | bytes 262144 | tf_op jit(solution)/shard_map/concatenate | solution.py:276
  2.4 0.5 collective-permute-start
  2.9 1.0 %collective-permute-done = f32[256,128]{1,0:T(8,128)S(1)} collective-permute-done((f32[256,128]{1,0:T(8,128)S(1)}, f32[256,128]{1,0:T(8,128)S(1)}, u32[]{:S(2)}, u32[]{:S(2)}) %collective-permute-start) | collective-permute-done | bytes 131104 | tf_op jit(solution)/shard_map/ppermute | solution.py:277
  3.9 0.9 %maximum_select_fusion.own_ref = f32[256,256]{1,0:T(8,128)S(1)} fusion(f32[256,128]{1,0:T(8,128)S(1)} %collective-permute-done, f32[128,128]{1,0:T(8,128)S(1)} %convert_element_type.5, f32[128,128]{1,0:T(8,128)} %param.18, pred[]{:T(512)S(6)} %eq.4), kind=kLoop, calls=%fused_computation | loop fusion | flops 327680 | bytes 524289 | tf_op jit(solution)/shard_map/jit(_where)/select_n | solution.py:278
  4.8 0.0 copy-start
  4.8 2.9 %collective-permute-start.1 = (f32[256,256]{1,0:T(8,128)S(1)}, f32[256,256]{1,0:T(8,128)S(1)}, u32[]{:S(2)}, u32[]{:S(2)}) collective-permute-start(f32[256,256]{1,0:T(8,128)S(1)} %maximum_select_fusion.own_ref), channel_id=1, source_target_pairs={{0,2},{2,4},{4,6},{6,8},{8,10},{10,12},{12,14},{14,15},{15,13},{13... | collective-permute-start | bytes 786440 | tf_op jit(solution)/shard_map/ppermute | solution.py:282
  7.8 1.6 %collective-permute-start.3 = (f32[192,256]{1,0:T(8,128)S(1)}, f32[192,256]{1,0:T(8,128)S(1)}, u32[]{:S(2)}, u32[]{:S(2)}) collective-permute-start(f32[192,256]{1,0:T(8,128)S(1)} %pad_maximum_fusion), channel_id=1, source_target_pairs={{0,4},{2,6},{4,8},{6,10},{8,12},{10,14},{12,15},{14,13},{15,11},{1... | collective-permute-start | bytes 589832 | tf_op jit(solution)/shard_map/ppermute | solution.py:283
  9.5 7.1 %collective-permute-done.1.s1_ref = f32[256,256]{1,0:T(8,128)S(1)} collective-permute-done((f32[256,256]{1,0:T(8,128)S(1)}, f32[256,256]{1,0:T(8,128)S(1)}, u32[]{:S(2)}, u32[]{:S(2)}) %collective-permute-start.1) | collective-permute-done | bytes 262176 | tf_op jit(solution)/shard_map/ppermute | solution.py:282
  16.6 0.0 copy-start.1
  16.6 0.0 collective-permute-start.2
  16.6 0.0 collective-permute-done.3.s2_ref
  16.6 0.0 copy-start.3
  16.6 0.5 collective-permute-start.4
  17.1 0.0 slice-done
  17.1 0.8 %pad.4 = f32[6,72,256]{2,1,0:T(8,128)} pad(f32[6,65,129]{2,1,0:T(8,128)S(1)} %slice-done, f32[]{:T(128)} %constant.43.clone.1), padding=0_0x0_7x0_127 | pad | bytes 643612 | tf_op jit(solution)/shard_map/jit(_pad)/pad | solution.py:249
  17.9 3.8 %spectra.1 = (f32[6,256,256]{2,1,0:T(8,128)}, f32[6,128,128]{2,1,0:T(8,128)}) custom-call(f32[432,256]{1,0:T(8,128)} %bitcast.3, bf16[256,384]{1,0:T(8,128)(2,1)} %constant.44.clone.rh_ref, bf16[256,384]{1,0:T(8,128)(2,1)} %constant.45.clone.rl_ref, bf16[256,72]{1,0:T(8,128)(2,1)} %constant.46.clone.ch_ref, bf16[256,72]{1,0:T(8,128)(2,1)} %constant.47.clone.cl_ref, ...), custom_call_target="tpu_custom_call" | custom-call | flops 679477248 | bytes 1572864 | tf_op jit(solution)/shard_map/spectra/pallas_call | solution.py:254
  21.8 0.0 copy-done
  21.8 0.0 copy-done.1
  21.8 0.0 copy-done.3
  21.8 0.6 %pad_add_fusion.where_ref = s32[3]{0:T(128)} fusion(s32[1]{0:T(128)} %constant.41.clone.1, s32[1]{0:T(128)} %bitcast.1, s32[1]{0:T(128)} %bitcast), kind=kLoop, calls=%fused_computation.4 | loop fusion | flops 6 | bytes 24 | tf_op jit(solution)/shard_map/stack | solution.py:287
  22.4 0.0 collective-permute-done.4.r2_ref
  22.4 0.0 copy-start.4
  22.4 0.0 collective-permute-done.2.r1_ref
  22.4 0.0 copy-start.2
  22.4 0.7 %copy-done.4 = f32[192,256]{1,0:T(8,128)} copy-done((f32[192,256]{1,0:T(8,128)}, f32[192,256]{1,0:T(8,128)S(1)}, u32[]{:S(2)}) %copy-start.4) | copy-done | bytes 196632
  23.1 0.1 copy-done.2
  23.2 16.3 %first_step.1 = (f32[384,256]{1,0:T(8,128)}, f32[384,128]{1,0:T(8,128)}, f32[256,128]{1,0:T(8,128)}) custom-call(s32[3]{0:T(128)} %pad_add_fusion.where_ref, f32[256,256]{1,0:T(8,128)} %copy-done, f32[256,256]{1,0:T(8,128)} %copy-done.1, f32[256,256]{1,0:T(8,128)} %copy-done.2, f32[192,256]{1,0:T(8,128)} %copy-done.3, f32[192,256]{1,0:T(8,128)} %copy-done.4, ...), custom_call_target="tpu_custom_call" | custom-call | tf_op jit(solution)/shard_map/first_step/pallas_call | solution.py:289
  39.4 0.1 collective-permute-start.5
  39.5 1.6 %collective-permute-done.5.got_ref = f32[384,128]{1,0:T(8,128)S(1)} collective-permute-done((f32[384,128]{1,0:T(8,128)}, f32[384,128]{1,0:T(8,128)S(1)}, u32[]{:S(2)}, u32[]{:S(2)}) %collective-permute-start.5) | collective-permute-done | bytes 196640 | tf_op jit(solution)/shard_map/ppermute | solution.py:298
  41.1 0.0 copy-start.5
  41.1 0.7 %copy-done.5 = f32[384,128]{1,0:T(8,128)} copy-done((f32[384,128]{1,0:T(8,128)}, f32[384,128]{1,0:T(8,128)S(1)}, u32[]{:S(2)}) %copy-start.5) | copy-done | bytes 196632
  41.8 12.0 %second_step.1 = (f32[128,128]{1,0:T(8,128)}, f32[128,128]{1,0:T(8,128)}, f32[128,128]{1,0:T(8,128)}) custom-call(s32[3]{0:T(128)} %pad_add_fusion.where_ref, f32[384,256]{1,0:T(8,128)} %get-tuple-element.12.rest_ref, f32[384,128]{1,0:T(8,128)} %copy-done.5, f32[256,128]{1,0:T(8,128)} %get-tuple-element.14.target_ref, ...), custom_call_target="tpu_custom_call" | custom-call | tf_op jit(solution)/shard_map/second_step/pallas_call | solution.py:299
  53.8 0.1 collective-permute-start.6
  53.9 1.3 %collective-permute-done.6 = f32[128,128]{1,0:T(8,128)S(1)} collective-permute-done((f32[128,128]{1,0:T(8,128)}, f32[128,128]{1,0:T(8,128)S(1)}, u32[]{:S(2)}, u32[]{:S(2)}) %collective-permute-start.6) | collective-permute-done | bytes 65568 | tf_op jit(solution)/shard_map/ppermute | solution.py:308
  55.2 1.5 %sub.3 = f32[128,128]{1,0:T(8,128)} subtract(f32[128,128]{1,0:T(8,128)} %get-tuple-element.15, f32[128,128]{1,0:T(8,128)S(1)} %collective-permute-done.6) | non-fusion elementwise | flops 16384 | bytes 196608 | tf_op jit(solution)/shard_map/sub | solution.py:308
  (3 shorter events, 0.0 us)
Async XLA Ops:
  0.6 16.5 %slice-start = ((f32[6,129,129]{2,1,0:T(8,128)}), f32[6,65,129]{2,1,0:T(8,128)S(1)}, s32[]{:S(2)}) async-start(f32[6,129,129]{2,1,0:T(8,128)} %param.20), calls=%async_computation | async-start | bytes 884736 | tf_op jit(solution)/shard_map/slice | solution.py:250
  2.4 1.5 %collective-permute-start = (f32[256,128]{1,0:T(8,128)S(1)}, f32[256,128]{1,0:T(8,128)S(1)}, u32[]{:S(2)}, u32[]{:S(2)}) collective-permute-start(f32[256,128]{1,0:T(8,128)S(1)} %pad_maximum_fusion.1), channel_id=1, source_target_pairs={{0,1},{1,0},{2,3},{3,2},{4,5},{5,4},{6,7},{7,6},{8,9},{9,8},{10,11... | collective-permute-start | bytes 393224 | tf_op jit(solution)/shard_map/ppermute | solution.py:277
  4.8 16.9 %copy-start = (f32[256,256]{1,0:T(8,128)}, f32[256,256]{1,0:T(8,128)S(1)}, u32[]{:S(2)}) copy-start(f32[256,256]{1,0:T(8,128)S(1)} %maximum_select_fusion.own_ref) | copy-start | bytes 786436
  4.8 11.7 %collective-permute-start.1 = (f32[256,256]{1,0:T(8,128)S(1)}, f32[256,256]{1,0:T(8,128)S(1)}, u32[]{:S(2)}, u32[]{:S(2)}) collective-permute-start(f32[256,256]{1,0:T(8,128)S(1)} %maximum_select_fusion.own_ref), channel_id=1, source_target_pairs={{0,2},{2,4},{4,6},{6,8},{8,10},{10,12},{12,14},{14,15},{15,13},{13... | collective-permute-start | bytes 786440 | tf_op jit(solution)/shard_map/ppermute | solution.py:282
  7.8 8.8 %collective-permute-start.3 = (f32[192,256]{1,0:T(8,128)S(1)}, f32[192,256]{1,0:T(8,128)S(1)}, u32[]{:S(2)}, u32[]{:S(2)}) collective-permute-start(f32[192,256]{1,0:T(8,128)S(1)} %pad_maximum_fusion), channel_id=1, source_target_pairs={{0,4},{2,6},{4,8},{6,10},{8,12},{10,14},{12,15},{14,13},{15,11},{1... | collective-permute-start | bytes 589832 | tf_op jit(solution)/shard_map/ppermute | solution.py:283
  16.6 5.2 %copy-start.1 = (f32[256,256]{1,0:T(8,128)}, f32[256,256]{1,0:T(8,128)S(1)}, u32[]{:S(2)}) copy-start(f32[256,256]{1,0:T(8,128)S(1)} %collective-permute-done.1.s1_ref) | copy-start | bytes 786436
  16.6 5.8 %collective-permute-start.2 = (f32[256,256]{1,0:T(8,128)S(1)}, f32[256,256]{1,0:T(8,128)S(1)}, u32[]{:S(2)}, u32[]{:S(2)}) collective-permute-start(f32[256,256]{1,0:T(8,128)S(1)} %collective-permute-done.1.s1_ref), channel_id=1, source_target_pairs={{0,1},{1,0},{2,3},{3,2},{4,5},{5,4},{6,7},{7,6},{8,9},{9,8},{10,11... | collective-permute-start | bytes 786440 | tf_op jit(solution)/shard_map/ppermute | solution.py:284
  16.6 5.2 %copy-start.3 = (f32[192,256]{1,0:T(8,128)}, f32[192,256]{1,0:T(8,128)S(1)}, u32[]{:S(2)}) copy-start(f32[192,256]{1,0:T(8,128)S(1)} %collective-permute-done.3.s2_ref) | copy-start | bytes 589828
  16.6 5.8 %collective-permute-start.4 = (f32[192,256]{1,0:T(8,128)S(1)}, f32[192,256]{1,0:T(8,128)S(1)}, u32[]{:S(2)}, u32[]{:S(2)}) collective-permute-start(f32[192,256]{1,0:T(8,128)S(1)} %collective-permute-done.3.s2_ref), channel_id=1, source_target_pairs={{0,1},{1,0},{2,3},{3,2},{4,5},{5,4},{6,7},{7,6},{8,9},{9,8},{10,11... | collective-permute-start | bytes 589832 | tf_op jit(solution)/shard_map/ppermute | solution.py:285
  22.4 0.7 %copy-start.4 = (f32[192,256]{1,0:T(8,128)}, f32[192,256]{1,0:T(8,128)S(1)}, u32[]{:S(2)}) copy-start(f32[192,256]{1,0:T(8,128)S(1)} %collective-permute-done.4.r2_ref) | copy-start | bytes 589828
  22.4 0.8 %copy-start.2 = (f32[256,256]{1,0:T(8,128)}, f32[256,256]{1,0:T(8,128)S(1)}, u32[]{:S(2)}) copy-start(f32[256,256]{1,0:T(8,128)S(1)} %collective-permute-done.2.r1_ref) | copy-start | bytes 786436
  39.4 1.7 %collective-permute-start.5 = (f32[384,128]{1,0:T(8,128)}, f32[384,128]{1,0:T(8,128)S(1)}, u32[]{:S(2)}, u32[]{:S(2)}) collective-permute-start(f32[384,128]{1,0:T(8,128)} %get-tuple-element.13), channel_id=1, source_target_pairs={{0,1},{1,0},{2,3},{3,2},{4,5},{5,4},{6,7},{7,6},{8,9},{9,8},{10,11... | collective-permute-start | bytes 589832 | tf_op jit(solution)/shard_map/ppermute | solution.py:298
  41.1 0.7 %copy-start.5 = (f32[384,128]{1,0:T(8,128)}, f32[384,128]{1,0:T(8,128)S(1)}, u32[]{:S(2)}) copy-start(f32[384,128]{1,0:T(8,128)S(1)} %collective-permute-done.5.got_ref) | copy-start | bytes 589828
  53.8 1.5 %collective-permute-start.6 = (f32[128,128]{1,0:T(8,128)}, f32[128,128]{1,0:T(8,128)S(1)}, u32[]{:S(2)}, u32[]{:S(2)}) collective-permute-start(f32[128,128]{1,0:T(8,128)} %get-tuple-element.16), channel_id=1, source_target_pairs={{0,1},{1,0},{2,3},{3,2},{4,5},{5,4},{6,7},{7,6},{8,9},{9,8},{10,11... | collective-permute-start | bytes 196616 | tf_op jit(solution)/shard_map/ppermute | solution.py:308
where the time goes:
time: 57 us; the launch traced here: 56.7 us
  Pallas kernels  32.1 us (56%)
  waiting for transfers between devices  11 us (19%)
  starting transfers between devices  5.8 us (10%)
  other arithmetic  4.83 us (8%)
  local copies, waits for them, and re-layouts  2.28 us (4%)
  between operations  0.7 us (1%)
    pallas_call x1, Pallas kernels, per_device(): pl.pallas_call(first_kernel, out_shape=(shape(3 * H, N), shape(3 * H, H),...  16.3 us
    pallas_call x1, Pallas kernels, per_device(): pl.pallas_call(second_kernel, out_shape=(shape(H, H), shape(H, H), shape(...  12 us
    ppermute x1, waiting for transfers between devices, per_device(): s1 = lax.ppermute(own, ('gx', 'gy'), ring(1))  7.12 us
    pallas_call x1, Pallas kernels, per_device(): pl.pallas_call(spectrum_kernel, out_shape=(shape(count, N, N), shape(coun...  3.85 us
    ppermute x1, starting transfers between devices, per_device(): s1 = lax.ppermute(own, ('gx', 'gy'), ring(1))  2.93 us
    ppermute x1, starting transfers between devices, per_device(): s2 = lax.ppermute(far, ('gx', 'gy'), ring(2))  1.63 us
    ppermute x1, waiting for transfers between devices, per_device(): got = lax.ppermute(send, 'gy', swap)  1.58 us
    sub x1, other arithmetic, per_device(): return (mask - lax.ppermute(send, 'gy', swap), resist)  1.48 us
  transfers between devices with their start and end apart: 7, of which 4 were waited for; matrix products, arithmetic and copies ran while one was open for 3% of the time, Pallas kernels for 7%

commit v1 on v0

v1 whole, which is shorter than its diff:
```python
import functools

import jax
import jax.numpy as jnp
import ml_dtypes
import numpy as np
from jax import lax
from jax.experimental import pallas as pl
from jax.experimental.pallas import tpu as pltpu
from jax.sharding import PartitionSpec as P

STEP = 0.1
STEEP = 4.0
THRESHOLD = 1.5
N = 256
H = 128
R = 64
VMEM = pl.BlockSpec(memory_space=pltpu.VMEM)


def stack(table, axis):
    high = table.astype(ml_dtypes.bfloat16)
    low = (table - high.astype(np.float64)).astype(ml_dtypes.bfloat16)
    return np.concatenate([high, low, high], axis)


def wave_tables():
    place = np.arange(N)
    freq = np.arange(H)
    angle = 2.0 * np.pi * ((freq[:, None] * place[None, :]) % N) / N
    forward = np.concatenate([np.cos(angle), np.sin(angle)], 0)
    forward[H] = np.where(place % 2 == 0, 1.0, -1.0)
    weight = np.full((N,), 2.0)
    weight[0] = weight[H] = 1.0
    inverse = (forward * weight[:, None] / N).T
    return forward, inverse


def spectrum_tables(size, rows):
    slot = np.arange(N)
    freq = np.where(slot < H, slot, np.where(slot == H, H, slot - H))
    b = np.arange(size) - (size - 1) // 2
    right = np.zeros((N, N + H))
    right[:size, :N] = np.cos(2.0 * np.pi * ((b[:, None] * freq[None, :]) % N) / N)
    right[:size, N:] = np.sin(2.0 * np.pi * ((b[:, None] * slot[None, :H]) % N) / N)
    a = np.arange((size + 1) // 2)
    fold = np.where(a == 0, 1.0, 2.0)
    left_cos = np.zeros((N, rows))
    left_cos[:, : a.size] = fold * np.cos(2.0 * np.pi * ((freq[:, None] * a[None, :]) % N) / N)
    left_sin = np.zeros((H, rows))
    left_sin[:, : a.size] = fold * np.sin(2.0 * np.pi * ((slot[:H, None] * a[None, :]) % N) / N)
    return right, left_cos, left_sin


def split(value):
    high = value.astype(jnp.bfloat16)
    low = (value - high.astype(jnp.float32)).astype(jnp.bfloat16)
    return high, low


def dot(left, right):
    return jnp.dot(left, right, preferred_element_type=jnp.float32)


def left(table, value):
    high, low = value
    return dot(table, jnp.concatenate([high, high, low], 0))


def right(value, table):
    high, low = value
    return dot(jnp.concatenate([high, high, low], 1), table)


def mix(f, p_ref, q_ref, k):
    q = q_ref[k]
    cc, cs, sc, ss = f[:H, :H], f[:H, H:], f[H:, :H], f[H:, H:]
    return jnp.concatenate(
        [
            jnp.concatenate(
                [p_ref[k, :H, :H] * cc + q * ss, p_ref[k, :H, H:] * cs - q * sc], 1
            ),
            jnp.concatenate(
                [p_ref[k, H:, :H] * sc - q * cs, p_ref[k, H:, H:] * ss + q * cc], 1
            ),
        ],
        0,
    )


def amplitudes(blocks, field, p_ref, q_ref, t, f_sc, a_sc, core):
    ey = split(right(split(field), t["fy"][...]))
    for b in range(blocks):
        rows = slice(b * H, b * H + N)
        f_sc[b] = left(t["fx"][...], (ey[0][rows], ey[1][rows]))
    for k in range(p_ref.shape[0]):
        for b in range(blocks):
            x = left(t["ix"][...], split(mix(f_sc[b], p_ref, q_ref, k)))
            a_sc[k, b * H : (b + 1) * H, :] = right(split(x), t["iy_own"][core])


def slopes(rows, count, a_sc, target, inside, w_sc):
    total = a_sc[0, :rows, :] * a_sc[0, :rows, :]
    for k in range(1, count):
        total = total + a_sc[k, :rows, :] * a_sc[k, :rows, :]
    resist = 1.0 / (1.0 + jnp.exp(-STEEP * (total - THRESHOLD)))
    slope = 2.0 * (resist - target) * STEEP * resist * (1.0 - resist)
    slope = jnp.where(inside, 2.0 * slope, 0.0)
    for k in range(count):
        high, low = split(a_sc[k, :rows, :] * slope)
        w_sc[k, :rows, :H] = high
        w_sc[k, :rows, H:] = low
    return resist


def gradients(blocks, p_ref, q_ref, t, w_sc, z_sc, core):
    rows = (blocks + 1) * H
    for k in range(p_ref.shape[0]):
        w = w_sc[k, :rows, :]
        high, low = split(dot(jnp.concatenate([w, w[:, :H]], 1), t["fy_own"][core]))
        for b in range(blocks):
            part = slice(b * H, b * H + N)
            z = mix(left(t["fx"][...], (high[part], low[part])), p_ref, q_ref, k)
            z_sc[b] = z if k == 0 else z_sc[b] + z
    return [
        right(split(left(t["ix"][...], split(z_sc[b]))), t["iy"][...]) for b in range(blocks)
    ]


def lane_mask(shape, core):
    lane = lax.broadcasted_iota(jnp.int32, shape, 1)
    return (lane >= core * R) & (lane < N - R + core * R)


def row_mask(shape, first, total):
    row = lax.broadcasted_iota(jnp.int32, shape, 0) + first
    return (row >= 0) & (row < total)


def spectrum_kernel(k_ref, right_ref, cos_ref, sin_ref, p_ref, q_ref):
    count = p_ref.shape[0]
    rows = k_ref.shape[0] // count
    section = right(split(k_ref[...]), right_ref[...])
    for k in range(count):
        high, low = split(section[k * rows : (k + 1) * rows])
        p_ref[k] = left(cos_ref[...], (high[:, :N], low[:, :N]))
        q_ref[k] = left(sin_ref[...], (high[:, N:], low[:, N:]))


TABLES = ("fx", "fy", "fy_own", "ix", "iy", "iy_own")


def first_kernel(tiles, own_ref, s1_ref, r1_ref, s2_ref, r2_ref, p_ref, q_ref, *refs):
    t = dict(zip(TABLES, refs))
    rest_ref, send_ref, target_ref, f_sc, a_sc, w_sc, z_sc = refs[len(TABLES) :]
    core, tile, total = lax.axis_index("gy"), lax.axis_index("gx"), tiles * H
    count = p_ref.shape[0]
    low1 = jnp.where(core == 0, s1_ref[...], r1_ref[...])
    upp1 = jnp.where(core == 0, r1_ref[...], s1_ref[...])
    low2 = jnp.where(core == 0, s2_ref[...], r2_ref[...])
    upp2 = jnp.where(core == 0, r2_ref[...], s2_ref[...])
    field = jnp.concatenate([low2[:H], low1[:H], own_ref[:H], upp1[:H], upp2[:H]], 0)
    inside = row_mask(field.shape, (tile - 2) * H, total) & lane_mask(field.shape, core)
    field = jnp.where(inside, field, 0.0)
    target = jnp.concatenate([low2[H:], low1[H:], own_ref[H:], upp1[H:], upp2[H:]], 0)
    target = jnp.where(core == 0, target[:, :H], target[:, H:])
    amplitudes(4, field, p_ref, q_ref, t, f_sc, a_sc, core)
    slopes(4 * H, count, a_sc, target, row_mask((4 * H, H), (tile - 1) * H - R, total), w_sc)
    target_ref[...] = target[H : 3 * H]
    for b, part in enumerate(gradients(3, p_ref, q_ref, t, w_sc, z_sc, core)):
        rows = slice(b * H, (b + 1) * H)
        rest_ref[rows, :] = field[(b + 1) * H : (b + 2) * H] - STEP * part
        send_ref[rows, :] = pltpu.roll(part, N - R, 1)[:, :H]


def second_kernel(tiles, rest_ref, got_ref, target_ref, p_ref, q_ref, *refs):
    t = dict(zip(TABLES, refs))
    mask_ref, send_ref, resist_ref, f_sc, a_sc, w_sc, z_sc = refs[len(TABLES) :]
    core, tile, total = lax.axis_index("gy"), lax.axis_index("gx"), tiles * H
    count = p_ref.shape[0]
    got = jnp.concatenate([got_ref[...], jnp.zeros_like(got_ref)], 1)
    field = rest_ref[...] - STEP * pltpu.roll(got, R, 1)
    inside = row_mask(field.shape, (tile - 1) * H, total) & lane_mask(field.shape, core)
    field = jnp.where(inside, field, 0.0)
    amplitudes(2, field, p_ref, q_ref, t, f_sc, a_sc, core)
    inside = row_mask((2 * H, H), tile * H - R, total)
    resist = slopes(2 * H, count, a_sc, target_ref[...], inside, w_sc)
    resist_ref[...] = resist[R : R + H]
    (part,) = gradients(1, p_ref, q_ref, t, w_sc, z_sc, core)
    part = jnp.where(lane_mask(part.shape, core), STEP * part, 0.0)
    own = field[H : 2 * H] - part
    mask_ref[...] = jnp.where(core == 0, own[:, :H], own[:, H:])
    send_ref[...] = jnp.where(core == 0, part[:, H:], part[:, :H])


def shape(*dims, dtype=jnp.float32):
    return jax.ShapeDtypeStruct(dims, dtype)


def scratch(blocks, adjoint_blocks, count):
    return [
        pltpu.VMEM((blocks, N, N), jnp.float32),
        pltpu.VMEM((count, blocks * H, H), jnp.float32),
        pltpu.VMEM((count, blocks * H, N), jnp.bfloat16),
        pltpu.VMEM((adjoint_blocks, N, N), jnp.float32),
    ]


def per_device(mask_init, target_map, kernels, tiles):
    count, size, _ = kernels.shape
    core = lax.axis_index("gy")
    tile = lax.axis_index("gx")
    swap = [(0, 1), (1, 0)]

    def place(step):
        step %= 2 * tiles
        return 2 * step if step < tiles else 2 * (2 * tiles - 1 - step) + 1

    def ring(shift):
        return [(place(i), place(i + shift)) for i in range(2 * tiles)]

    rows = 72
    half = jnp.pad(
        kernels[:, (size - 1) // 2 :, :],
        ((0, 0), (0, rows - (size + 1) // 2), (0, N - size)),
    ).reshape(count * rows, N)
    right_table, left_cos, left_sin = spectrum_tables(size, rows)
    spectral = [stack(right_table, 0), stack(left_cos, 1), stack(left_sin, 1)]
    spectral = [jnp.asarray(v) for v in spectral]
    p, q = pl.pallas_call(
        spectrum_kernel,
        out_shape=(shape(count, N, N), shape(count, H, H)),
        in_specs=[VMEM] * 4,
        out_specs=(VMEM, VMEM),
        cost_estimate=pl.CostEstimate(
            flops=6 * count * rows * N * N * 4, bytes_accessed=4 * count * N * N, transcendentals=0
        ),
        compiler_params=pltpu.CompilerParams(vmem_limit_bytes=12 << 20),
        name="spectra",
    )(half, *spectral)

    forward, inverse = wave_tables()
    halves = [slice(c, c + H) for c in (0, H)]
    tables = [
        stack(forward, 1),
        stack(forward.T, 0),
        np.stack([np.roll(stack(forward.T[c], 0), H, 0) for c in halves]),
        stack(inverse[R : R + H], 1),
        stack(inverse.T, 0),
        np.stack([stack(inverse.T[:, c], 0) for c in halves]),
    ]
    tables = [jnp.asarray(v) for v in tables]

    mine = jnp.concatenate([mask_init, target_map.astype(jnp.float32)], 0)
    mate = lax.ppermute(mine, "gy", swap)
    own = jnp.where(
        core == 0, jnp.concatenate([mine, mate], 1), jnp.concatenate([mate, mine], 1)
    )
    far = jnp.concatenate([own[:H], jnp.where(core == 0, own[H + R :], own[H : H + R])], 0)
    s1 = lax.ppermute(own, ("gx", "gy"), ring(1))
    s2 = lax.ppermute(far, ("gx", "gy"), ring(2))
    r1 = lax.ppermute(s1, "gy", swap)
    r2 = lax.ppermute(s2, "gy", swap)

    params = pltpu.CompilerParams(vmem_limit_bytes=40 << 20)
    rest, send, target = pl.pallas_call(
        functools.partial(first_kernel, tiles),
        out_shape=(shape(3 * H, N), shape(3 * H, H), shape(2 * H, H)),
        in_specs=[VMEM] * (7 + len(tables)),
        out_specs=(VMEM,) * 3,
        scratch_shapes=scratch(4, 3, count),
        compiler_params=params,
        name="first_step",
    )(own, s1, r1, s2, r2, p, q, *tables)
    got = lax.ppermute(send, "gy", swap)
    mask, send, resist = pl.pallas_call(
        functools.partial(second_kernel, tiles),
        out_shape=(shape(H, H), shape(H, H), shape(H, H)),
        in_specs=[VMEM] * (5 + len(tables)),
        out_specs=(VMEM,) * 3,
        scratch_shapes=scratch(2, 1, count),
        compiler_params=params,
        name="second_step",
    )(rest, got, target, p, q, *tables)
    return mask - lax.ppermute(send, "gy", swap), resist


def solution(mesh):
    spec = P(("win", "gx"), "gy")
    return jax.shard_map(
        functools.partial(per_device, tiles=mesh.shape["gx"]),
        mesh=mesh,
        in_specs=(spec, spec, P()),
        out_specs=(spec, spec),
        check_vma=False,
    )
```

time: 57 us -> 37.5 us (0.66)
  Pallas kernels: 32.1 us -> 16.1 us
  local copies, waits for them, and re-layouts: 2.28 us -> 0.29 us
  other arithmetic: 4.83 us -> 3.35 us
    pallas_call x2, Pallas kernels: 28.2 us -> 15.2 us  [the longest x1 9.86 us: per_device(): pl.pallas_call(functools.partial(first_kernel, tiles), out_shape=(shape(3...]
    pallas_call x1, Pallas kernels: 3.85 us -> 0.9 us  [per_device(): pl.pallas_call(spectrum_kernel, out_shape=(shape(count, N, N), shape(coun...]
    unnamed x12 -> x18, local copies, waits for them, and re-layouts: 1.46 us -> 0.24 us
    sub x1, other arithmetic: 1.48 us -> 0.64 us  [per_device(): return (mask - lax.ppermute(send, 'gy', swap), resist)]
    pad x1, local copies, waits for them, and re-layouts: 0.8 us -> 0.03 us  [per_device(): jnp.pad(kernels[:, (size - 1) // 2:, :], ((0, 0), (0, rows - (size + 1) /...]
    another operation x1 -> x0, other arithmetic: 0.65 us -> none  [per_device(): where = jnp.stack([core, tile, jnp.int32(tiles * H)]).astype(jnp.int32)]
  transfers between devices with their start and end apart: 7 -> 7, of which waited for: 4 -> 5; matrix products, arithmetic and copies ran while one was open for 3% -> 0% of each run, Pallas kernels for 7% -> 2%
where the time goes in v1:
time: 37.5 us; the launch traced here: 37.2 us
  Pallas kernels  16.1 us (43%)
  waiting for transfers between devices  10.9 us (29%)
  starting transfers between devices  5.8 us (15%)
  other arithmetic  3.35 us (9%)
  between operations  0.77 us (2%)
    pallas_call x1, Pallas kernels, per_device(): pl.pallas_call(functools.partial(first_kernel, tiles), out_shape=(shape(3...  9.86 us
    ppermute x1, waiting for transfers between devices, per_device(): s1 = lax.ppermute(own, ('gx', 'gy'), ring(1))  7.12 us
    pallas_call x1, Pallas kernels, per_device(): pl.pallas_call(functools.partial(second_kernel, tiles), out_shape=(shape(...  5.35 us
    ppermute x1, starting transfers between devices, per_device(): s1 = lax.ppermute(own, ('gx', 'gy'), ring(1))  2.93 us
    ppermute x1, starting transfers between devices, per_device(): s2 = lax.ppermute(far, ('gx', 'gy'), ring(2))  1.63 us
    ppermute x1, waiting for transfers between devices, per_device(): got = lax.ppermute(send, 'gy', swap)  1.43 us
    ppermute x1, waiting for transfers between devices, per_device(): return (mask - lax.ppermute(send, 'gy', swap), resist)  1.12 us
    ppermute x1, waiting for transfers between devices, per_device(): mate = lax.ppermute(mine, 'gy', swap)  0.98 us
  transfers between devices with their start and end apart: 7, of which 5 were waited for; matrix products, arithmetic and copies ran while one was open for 0% of the time, Pallas kernels for 2%

profile of v1, /device:TPU:0, one launch (start us, length us, event | category | flops | bytes accessed | tf_op | source)
XLA Modules:
  0.0 37.2 jit_solution(9491913674183441694)
XLA Ops:
  0.6 0.0 slice-start
  0.6 0.9 %convert_element_type.5 = f32[128,128]{1,0:T(8,128)S(1)} convert(s32[128,128]{1,0:T(8,128)} %param.13) | non-fusion elementwise | flops 16384 | bytes 131072 | tf_op jit(solution)/shard_map/convert_element_type | solution.py:254
  1.5 0.8 %pad_maximum_fusion.1 = f32[256,128]{1,0:T(8,128)S(1)} fusion(f32[128,128]{1,0:T(8,128)S(1)} %convert_element_type.5, f32[128,128]{1,0:T(8,128)} %param.12), kind=kLoop, calls=%fused_computation.2 | loop fusion | flops 32768 | bytes 262144 | tf_op jit(solution)/shard_map/concatenate | solution.py:254
  2.4 0.5 %collective-permute-start = (f32[256,128]{1,0:T(8,128)S(1)}, f32[256,128]{1,0:T(8,128)S(1)}, u32[]{:S(2)}, u32[]{:S(2)}) collective-permute-start(f32[256,128]{1,0:T(8,128)S(1)} %pad_maximum_fusion.1), channel_id=1, source_target_pairs={{0,1},{1,0},{2,3},{3,2},{4,5},{5,4},{6,7},{7,6},{8,9},{9,8},{10,11... | collective-permute-start | bytes 393224 | tf_op jit(solution)/shard_map/ppermute | solution.py:255
  2.9 0.0 copy-start.6
  2.9 0.0 copy-start.7
  2.9 0.0 copy-start.8
  2.9 1.0 %collective-permute-done = f32[256,128]{1,0:T(8,128)S(1)} collective-permute-done((f32[256,128]{1,0:T(8,128)S(1)}, f32[256,128]{1,0:T(8,128)S(1)}, u32[]{:S(2)}, u32[]{:S(2)}) %collective-permute-start) | collective-permute-done | bytes 131104 | tf_op jit(solution)/shard_map/ppermute | solution.py:255
  3.9 0.9 %maximum_select_fusion.own_ref = f32[256,256]{1,0:T(8,128)S(1)} fusion(f32[256,128]{1,0:T(8,128)S(1)} %collective-permute-done, f32[128,128]{1,0:T(8,128)S(1)} %convert_element_type.5, f32[128,128]{1,0:T(8,128)} %param.12, pred[]{:T(512)S(6)} %eq.4), kind=kLoop, calls=%fused_computation | loop fusion | flops 327680 | bytes 524289 | tf_op jit(solution)/shard_map/jit(_where)/select_n | solution.py:256
  4.8 2.9 %collective-permute-start.1 = (f32[256,256]{1,0:T(8,128)S(1)}, f32[256,256]{1,0:T(8,128)S(1)}, u32[]{:S(2)}, u32[]{:S(2)}) collective-permute-start(f32[256,256]{1,0:T(8,128)S(1)} %maximum_select_fusion.own_ref), channel_id=1, source_target_pairs={{0,2},{2,4},{4,6},{6,8},{8,10},{10,12},{12,14},{14,15},{15,13},{13... | collective-permute-start | bytes 786440 | tf_op jit(solution)/shard_map/ppermute | solution.py:260
  7.8 1.6 %collective-permute-start.3 = (f32[192,256]{1,0:T(8,128)S(1)}, f32[192,256]{1,0:T(8,128)S(1)}, u32[]{:S(2)}, u32[]{:S(2)}) collective-permute-start(f32[192,256]{1,0:T(8,128)S(1)} %pad_maximum_fusion), channel_id=1, source_target_pairs={{0,4},{2,6},{4,8},{6,10},{8,12},{10,14},{12,15},{14,13},{15,11},{1... | collective-permute-start | bytes 589832 | tf_op jit(solution)/shard_map/ppermute | solution.py:261
  9.5 7.1 %collective-permute-done.1.s1_ref = f32[256,256]{1,0:T(8,128)S(1)} collective-permute-done((f32[256,256]{1,0:T(8,128)S(1)}, f32[256,256]{1,0:T(8,128)S(1)}, u32[]{:S(2)}, u32[]{:S(2)}) %collective-permute-start.1) | collective-permute-done | bytes 262176 | tf_op jit(solution)/shard_map/ppermute | solution.py:260
  16.6 0.0 collective-permute-start.2
  16.6 0.0 collective-permute-done.3.s2_ref
  16.6 0.5 %collective-permute-start.4 = (f32[192,256]{1,0:T(8,128)S(1)}, f32[192,256]{1,0:T(8,128)S(1)}, u32[]{:S(2)}, u32[]{:S(2)}) collective-permute-start(f32[192,256]{1,0:T(8,128)S(1)} %collective-permute-done.3.s2_ref), channel_id=1, source_target_pairs={{0,1},{1,0},{2,3},{3,2},{4,5},{5,4},{6,7},{7,6},{8,9},{9,8},{10,11... | collective-permute-start | bytes 589832 | tf_op jit(solution)/shard_map/ppermute | solution.py:263
  17.1 0.0 slice-done
  17.1 0.0 copy-start
  17.1 0.0 copy-start.1
  17.1 0.0 copy-start.2
  17.1 0.0 copy-start.3
  17.1 0.0 copy-start.4
  17.1 0.0 copy-start.5
  17.2 0.0 copy-done.6
  17.2 0.0 copy-done.7
  17.2 0.0 copy-done.8
  17.2 0.9 %spectra.1 = (f32[6,256,256]{2,1,0:T(8,128)S(1)}, f32[6,128,128]{2,1,0:T(8,128)S(1)}) custom-call(f32[432,256]{1,0:T(8,128)S(1)} %bitcast.1, bf16[768,384]{1,0:T(8,128)(2,1)S(1)} %copy-done.6, bf16[256,216]{1,0:T(8,128)(2,1)S(1)} %copy-done.7, bf16[128,216]{1,0:T(8,128)(2,1)S(1)} %copy-done.8), custom_call_target="tpu_custom_call" | custom-call | flops 679477248 | bytes 1572864 | tf_op jit(solution)/shard_map/spectra/pallas_call | solution.py:230
  18.1 0.3 collective-permute-done.4.r2_ref
  18.4 0.0 collective-permute-done.2.r1_ref
  18.4 0.0 copy-done
  18.4 0.0 copy-done.1
  18.4 0.0 copy-done.2
  18.4 0.0 copy-done.3
  18.4 0.1 copy-done.4
  18.6 0.0 copy-done.5
  18.6 9.9 %first_step.1 = (f32[384,256]{1,0:T(8,128)S(1)}, f32[384,128]{1,0:T(8,128)S(1)}, f32[256,128]{1,0:T(8,128)S(1)}) custom-call(f32[256,256]{1,0:T(8,128)S(1)} %maximum_select_fusion.own_ref, f32[256,256]{1,0:T(8,128)S(1)} %collective-permute-done.1.s1_ref, f32[256,256]{1,0:T(8,128)S(1)} %collective-permute-done.2.r1_ref, ...), custom_call_target="tpu_custom_call" | custom-call | tf_op jit(solution)/shard_map/first_step/pallas_call | solution.py:266
  28.5 0.1 collective-permute-start.5
  28.6 1.4 %collective-permute-done.5.got_ref = f32[384,128]{1,0:T(8,128)S(1)} collective-permute-done((f32[384,128]{1,0:T(8,128)S(1)}, f32[384,128]{1,0:T(8,128)S(1)}, u32[]{:S(2)}, u32[]{:S(2)}) %collective-permute-start.5) | collective-permute-done | bytes 196640 | tf_op jit(solution)/shard_map/ppermute | solution.py:275
  30.0 5.3 %second_step.1 = (f32[128,128]{1,0:T(8,128)S(1)}, f32[128,128]{1,0:T(8,128)S(1)}, f32[128,128]{1,0:T(8,128)}) custom-call(f32[384,256]{1,0:T(8,128)S(1)} %get-tuple-element.12.rest_ref, f32[384,128]{1,0:T(8,128)S(1)} %collective-permute-done.5.got_ref, f32[256,128]{1,0:T(8,128)S(1)} %get-tuple-element.14.target_ref, ...), custom_call_target="tpu_custom_call" | custom-call | tf_op jit(solution)/shard_map/second_step/pallas_call | solution.py:276
  35.3 0.1 collective-permute-start.6
  35.5 1.1 %collective-permute-done.6 = f32[128,128]{1,0:T(8,128)S(1)} collective-permute-done((f32[128,128]{1,0:T(8,128)S(1)}, f32[128,128]{1,0:T(8,128)S(1)}, u32[]{:S(2)}, u32[]{:S(2)}) %collective-permute-start.6) | collective-permute-done | bytes 65568 | tf_op jit(solution)/shard_map/ppermute | solution.py:285
  36.6 0.6 %sub.3 = f32[128,128]{1,0:T(8,128)} subtract(f32[128,128]{1,0:T(8,128)S(1)} %get-tuple-element.15, f32[128,128]{1,0:T(8,128)S(1)} %collective-permute-done.6) | non-fusion elementwise | flops 16384 | bytes 196608 | tf_op jit(solution)/shard_map/sub | solution.py:285
  (4 shorter events, 0.1 us)
Async XLA Ops:
  0.6 16.5 %slice-start = ((f32[6,129,129]{2,1,0:T(8,128)}), f32[6,65,129]{2,1,0:T(8,128)S(1)}, s32[]{:S(2)}) async-start(f32[6,129,129]{2,1,0:T(8,128)} %param.14), calls=%async_computation | async-start | bytes 884736 | tf_op jit(solution)/shard_map/slice | solution.py:224
  2.4 1.5 %collective-permute-start = (f32[256,128]{1,0:T(8,128)S(1)}, f32[256,128]{1,0:T(8,128)S(1)}, u32[]{:S(2)}, u32[]{:S(2)}) collective-permute-start(f32[256,128]{1,0:T(8,128)S(1)} %pad_maximum_fusion.1), channel_id=1, source_target_pairs={{0,1},{1,0},{2,3},{3,2},{4,5},{5,4},{6,7},{7,6},{8,9},{9,8},{10,11... | collective-permute-start | bytes 393224 | tf_op jit(solution)/shard_map/ppermute | solution.py:255
  2.9 14.3 %copy-start.6 = (bf16[768,384]{1,0:T(8,128)(2,1)S(1)}, bf16[768,384]{1,0:T(8,128)(2,1)}, u32[]{:S(2)}) copy-start(bf16[768,384]{1,0:T(8,128)(2,1)} %constant.26.clone.right_ref) | copy-start | bytes 1769476
  2.9 14.3 %copy-start.7 = (bf16[256,216]{1,0:T(8,128)(2,1)S(1)}, bf16[256,216]{1,0:T(8,128)(2,1)}, u32[]{:S(2)}) copy-start(bf16[256,216]{1,0:T(8,128)(2,1)} %constant.27.clone.cos_ref) | copy-start | bytes 331780
  2.9 14.3 %copy-start.8 = (bf16[128,216]{1,0:T(8,128)(2,1)S(1)}, bf16[128,216]{1,0:T(8,128)(2,1)}, u32[]{:S(2)}) copy-start(bf16[128,216]{1,0:T(8,128)(2,1)} %constant.28.clone.sin_ref) | copy-start | bytes 165892
  4.8 11.7 %collective-permute-start.1 = (f32[256,256]{1,0:T(8,128)S(1)}, f32[256,256]{1,0:T(8,128)S(1)}, u32[]{:S(2)}, u32[]{:S(2)}) collective-permute-start(f32[256,256]{1,0:T(8,128)S(1)} %maximum_select_fusion.own_ref), channel_id=1, source_target_pairs={{0,2},{2,4},{4,6},{6,8},{8,10},{10,12},{12,14},{14,15},{15,13},{13... | collective-permute-start | bytes 786440 | tf_op jit(solution)/shard_map/ppermute | solution.py:260
  7.8 8.8 %collective-permute-start.3 = (f32[192,256]{1,0:T(8,128)S(1)}, f32[192,256]{1,0:T(8,128)S(1)}, u32[]{:S(2)}, u32[]{:S(2)}) collective-permute-start(f32[192,256]{1,0:T(8,128)S(1)} %pad_maximum_fusion), channel_id=1, source_target_pairs={{0,4},{2,6},{4,8},{6,10},{8,12},{10,14},{12,15},{14,13},{15,11},{1... | collective-permute-start | bytes 589832 | tf_op jit(solution)/shard_map/ppermute | solution.py:261
  16.6 1.8 %collective-permute-start.2 = (f32[256,256]{1,0:T(8,128)S(1)}, f32[256,256]{1,0:T(8,128)S(1)}, u32[]{:S(2)}, u32[]{:S(2)}) collective-permute-start(f32[256,256]{1,0:T(8,128)S(1)} %collective-permute-done.1.s1_ref), channel_id=1, source_target_pairs={{0,1},{1,0},{2,3},{3,2},{4,5},{5,4},{6,7},{7,6},{8,9},{9,8},{10,11... | collective-permute-start | bytes 786440 | tf_op jit(solution)/shard_map/ppermute | solution.py:262
  16.6 1.8 %collective-permute-start.4 = (f32[192,256]{1,0:T(8,128)S(1)}, f32[192,256]{1,0:T(8,128)S(1)}, u32[]{:S(2)}, u32[]{:S(2)}) collective-permute-start(f32[192,256]{1,0:T(8,128)S(1)} %collective-permute-done.3.s2_ref), channel_id=1, source_target_pairs={{0,1},{1,0},{2,3},{3,2},{4,5},{5,4},{6,7},{7,6},{8,9},{9,8},{10,11... | collective-permute-start | bytes 589832 | tf_op jit(solution)/shard_map/ppermute | solution.py:263
  17.1 1.3 %copy-start = (bf16[2,768,128]{2,1,0:T(8,128)(2,1)S(1)}, bf16[2,768,128]{2,1,0:T(8,128)(2,1)}, u32[]{:S(2)}) copy-start(bf16[2,768,128]{2,1,0:T(8,128)(2,1)} %constant.34.clone.refs_5_) | copy-start | bytes 1179652
  17.1 1.3 %copy-start.1 = (bf16[768,256]{1,0:T(8,128)(2,1)S(1)}, bf16[768,256]{1,0:T(8,128)(2,1)}, u32[]{:S(2)}) copy-start(bf16[768,256]{1,0:T(8,128)(2,1)} %constant.33.clone.refs_4_) | copy-start | bytes 1179652
  17.1 1.3 %copy-start.2 = (bf16[2,384,256]{2,1,0:T(8,128)(2,1)S(1)}, bf16[2,384,256]{2,1,0:T(8,128)(2,1)}, u32[]{:S(2)}) copy-start(bf16[2,384,256]{2,1,0:T(8,128)(2,1)} %constant.31.clone.refs_2_) | copy-start | bytes 1179652
  17.1 1.3 %copy-start.3 = (bf16[768,256]{1,0:T(8,128)(2,1)S(1)}, bf16[768,256]{1,0:T(8,128)(2,1)}, u32[]{:S(2)}) copy-start(bf16[768,256]{1,0:T(8,128)(2,1)} %constant.30.clone.refs_1_) | copy-start | bytes 1179652
  17.1 1.5 %copy-start.4 = (bf16[256,768]{1,0:T(8,128)(2,1)S(1)}, bf16[256,768]{1,0:T(8,128)(2,1)}, u32[]{:S(2)}) copy-start(bf16[256,768]{1,0:T(8,128)(2,1)} %constant.29.clone.refs_0_) | copy-start | bytes 1179652
  17.1 1.5 %copy-start.5 = (bf16[128,768]{1,0:T(8,128)(2,1)S(1)}, bf16[128,768]{1,0:T(8,128)(2,1)}, u32[]{:S(2)}) copy-start(bf16[128,768]{1,0:T(8,128)(2,1)} %constant.32.clone.refs_3_) | copy-start | bytes 589828
  28.5 1.5 %collective-permute-start.5 = (f32[384,128]{1,0:T(8,128)S(1)}, f32[384,128]{1,0:T(8,128)S(1)}, u32[]{:S(2)}, u32[]{:S(2)}) collective-permute-start(f32[384,128]{1,0:T(8,128)S(1)} %get-tuple-element.13), channel_id=1, source_target_pairs={{0,1},{1,0},{2,3},{3,2},{4,5},{5,4},{6,7},{7,6},{8,9},{9,8},{10,11... | collective-permute-start | bytes 589832 | tf_op jit(solution)/shard_map/ppermute | solution.py:275
  35.3 1.3 %collective-permute-start.6 = (f32[128,128]{1,0:T(8,128)S(1)}, f32[128,128]{1,0:T(8,128)S(1)}, u32[]{:S(2)}, u32[]{:S(2)}) collective-permute-start(f32[128,128]{1,0:T(8,128)S(1)} %get-tuple-element.16), channel_id=1, source_target_pairs={{0,1},{1,0},{2,3},{3,2},{4,5},{5,4},{6,7},{7,6},{8,9},{9,8},{10,11... | collective-permute-start | bytes 196616 | tf_op jit(solution)/shard_map/ppermute | solution.py:285

commit v2 on v1

--- a/solution.py
+++ b/solution.py
@@ -24,32 +24,26 @@
     return np.concatenate([high, low, high], axis)
 
 
+def waves(freqs, places):
+    angle = np.pi / N * ((2 * freqs + 1) * places % (2 * N))
+    return np.cos(angle), np.sin(angle)
+
+
 def wave_tables():
-    place = np.arange(N)
+    forward = np.concatenate(waves(np.arange(H)[:, None], np.arange(N)[None, :]), 0)
+    return forward, forward.T * (2.0 / N)
+
+
+def spectrum_tables(size, rows):
     freq = np.arange(H)
-    angle = 2.0 * np.pi * ((freq[:, None] * place[None, :]) % N) / N
-    forward = np.concatenate([np.cos(angle), np.sin(angle)], 0)
-    forward[H] = np.where(place % 2 == 0, 1.0, -1.0)
-    weight = np.full((N,), 2.0)
-    weight[0] = weight[H] = 1.0
-    inverse = (forward * weight[:, None] / N).T
-    return forward, inverse
-
-
-def spectrum_tables(size, rows):
-    slot = np.arange(N)
-    freq = np.where(slot < H, slot, np.where(slot == H, H, slot - H))
-    b = np.arange(size) - (size - 1) // 2
-    right = np.zeros((N, N + H))
-    right[:size, :N] = np.cos(2.0 * np.pi * ((b[:, None] * freq[None, :]) % N) / N)
-    right[:size, N:] = np.sin(2.0 * np.pi * ((b[:, None] * slot[None, :H]) % N) / N)
-    a = np.arange((size + 1) // 2)
-    fold = np.where(a == 0, 1.0, 2.0)
-    left_cos = np.zeros((N, rows))
-    left_cos[:, : a.size] = fold * np.cos(2.0 * np.pi * ((freq[:, None] * a[None, :]) % N) / N)
-    left_sin = np.zeros((H, rows))
-    left_sin[:, : a.size] = fold * np.sin(2.0 * np.pi * ((slot[:H, None] * a[None, :]) % N) / N)
-    return right, left_cos, left_sin
+    places = np.arange(size) - (size - 1) // 2
+    right = np.zeros((N, N))
+    right[:size] = np.concatenate(waves(freq[None, :], places[:, None]), 1)
+    below = np.arange((size + 1) // 2)
+    left = np.zeros((2, H, rows))
+    left[:, :, : below.size] = waves(freq[:, None], below[None, :])
+    left[:, :, 1:] *= 2.0
+    return right, left[0], left[1]
 
 
 def split(value):
@@ -72,59 +66,99 @@
     return dot(jnp.concatenate([high, high, low], 1), table)
 
 
-def mix(f, p_ref, q_ref, k):
-    q = q_ref[k]
-    cc, cs, sc, ss = f[:H, :H], f[:H, H:], f[H:, :H], f[H:, H:]
-    return jnp.concatenate(
-        [
-            jnp.concatenate(
-                [p_ref[k, :H, :H] * cc + q * ss, p_ref[k, :H, H:] * cs - q * sc], 1
-            ),
-            jnp.concatenate(
-                [p_ref[k, H:, :H] * sc - q * cs, p_ref[k, H:, H:] * ss + q * cc], 1
-            ),
-        ],
-        0,
-    )
-
-
-def amplitudes(blocks, field, p_ref, q_ref, t, f_sc, a_sc, core):
+def mix(f, p, q, rows):
+    upper = slice(rows.start, rows.stop)
+    lower = slice(H + rows.start, H + rows.stop)
+    cc, cs, sc, ss = f[upper, :H], f[upper, H:], f[lower, :H], f[lower, H:]
+    p, q = p[rows], q[rows]
+    return p * cc + q * ss, p * cs - q * sc, p * sc - q * cs, p * ss + q * cc
+
+
+def store_quarters(ref, rows, quarters):
+    lower = slice(H + rows.start, H + rows.stop)
+    places = ((rows, slice(0, H)), (rows, slice(H, N)), (lower, slice(0, H)), (lower, slice(H, N)))
+    for (x, y), quarter in zip(places, quarters):
+        ref[0, x, y], ref[1, x, y] = split(quarter)
+
+
+CHUNKS = [slice(r, r + 16) for r in range(0, H, 16)]
+
+
+def pipeline(count, *stages):
+    for step in range(count + len(stages) - 1):
+        for lag, stage in enumerate(reversed(stages)):
+            item = step - (len(stages) - 1 - lag)
+            if 0 <= item < count:
+                stage(item)
+
+
+def amplitudes(blocks, field, p_ref, q_ref, t, f_sc, g_sc, x_sc, a_sc, core):
     ey = split(right(split(field), t["fy"][...]))
     for b in range(blocks):
         rows = slice(b * H, b * H + N)
         f_sc[b] = left(t["fx"][...], (ey[0][rows], ey[1][rows]))
-    for k in range(p_ref.shape[0]):
-        for b in range(blocks):
-            x = left(t["ix"][...], split(mix(f_sc[b], p_ref, q_ref, k)))
-            a_sc[k, b * H : (b + 1) * H, :] = right(split(x), t["iy_own"][core])
-
-
-def slopes(rows, count, a_sc, target, inside, w_sc):
-    total = a_sc[0, :rows, :] * a_sc[0, :rows, :]
-    for k in range(1, count):
-        total = total + a_sc[k, :rows, :] * a_sc[k, :rows, :]
-    resist = 1.0 / (1.0 + jnp.exp(-STEEP * (total - THRESHOLD)))
-    slope = 2.0 * (resist - target) * STEEP * resist * (1.0 - resist)
-    slope = jnp.where(inside, 2.0 * slope, 0.0)
-    for k in range(count):
-        high, low = split(a_sc[k, :rows, :] * slope)
-        w_sc[k, :rows, :H] = high
-        w_sc[k, :rows, H:] = low
-    return resist
-
-
-def gradients(blocks, p_ref, q_ref, t, w_sc, z_sc, core):
-    rows = (blocks + 1) * H
-    for k in range(p_ref.shape[0]):
-        w = w_sc[k, :rows, :]
-        high, low = split(dot(jnp.concatenate([w, w[:, :H]], 1), t["fy_own"][core]))
-        for b in range(blocks):
-            part = slice(b * H, b * H + N)
-            z = mix(left(t["fx"][...], (high[part], low[part])), p_ref, q_ref, k)
-            z_sc[b] = z if k == 0 else z_sc[b] + z
-    return [
-        right(split(left(t["ix"][...], split(z_sc[b]))), t["iy"][...]) for b in range(blocks)
-    ]
+
+    def mixed(i):
+        k, b = i // blocks, i % blocks
+        for rows in CHUNKS:
+            quarters = mix(f_sc.at[b], p_ref.at[k], q_ref.at[k], rows)
+            store_quarters(g_sc.at[i], rows, quarters)
+
+    def inverse_x(i):
+        x = left(t["ix"][...], (g_sc[i, 0], g_sc[i, 1]))
+        x_sc[0, i], x_sc[1, i] = split(x)
+
+    def inverse_y(i):
+        k, b = i // blocks, i % blocks
+        a_sc[k, b * H : (b + 1) * H, :] = right((x_sc[0, i], x_sc[1, i]), t["iy_own"][core])
+
+    pipeline(p_ref.shape[0] * blocks, mixed, inverse_x, inverse_y)
+
+
+def slopes(blocks, count, a_sc, target, inside, w_sc):
+    resists = []
+    for c in range(0, blocks * H, R):
+        rows = slice(c, c + R)
+        amplitude = [a_sc[k, rows, :] for k in range(count)]
+        total = amplitude[0] * amplitude[0]
+        for k in range(1, count):
+            total = total + amplitude[k] * amplitude[k]
+        resist = 1.0 / (1.0 + jnp.exp(-STEEP * (total - THRESHOLD)))
+        slope = 2.0 * (resist - target[rows]) * STEEP * resist * (1.0 - resist)
+        slope = jnp.where(inside[rows], 2.0 * slope, 0.0)
+        for k in range(count):
+            cols = slice(k * H, (k + 1) * H)
+            w_sc[0, rows, cols], w_sc[1, rows, cols] = split(amplitude[k] * slope)
+        resists.append(resist)
+    return resists
+
+
+def gradients(blocks, count, p_ref, q_ref, t, w_sc, y_sc, u_sc, z_sc, core):
+    def forward_x(b):
+        rows = slice(b * H, b * H + N)
+        y = left(t["fx"][...], (w_sc[0, rows, :], w_sc[1, rows, :]))
+        y_sc[0, b], y_sc[1, b] = split(y)
+
+    def forward_y(b):
+        for k in range(count):
+            cols = slice(k * H, (k + 1) * H)
+            u_sc[b, k] = right((y_sc[0, b, :, cols], y_sc[1, b, :, cols]), t["fy_own"][core])
+
+    def mixed(b):
+        for rows in CHUNKS:
+            terms = [mix(u_sc.at[b, k], p_ref.at[k], q_ref.at[k], rows) for k in range(count)]
+            store_quarters(z_sc.at[b], rows, [sum(quarter) for quarter in zip(*terms)])
+
+    def inverse_x(b):
+        y_sc[0, b, :H, :N], y_sc[1, b, :H, :N] = split(left(t["ix"][...], (z_sc[b, 0], z_sc[b, 1])))
+
+    out = []
+
+    def inverse_y(b):
+        out.append(right((y_sc[0, b, :H, :N], y_sc[1, b, :H, :N]), t["iy"][...]))
+
+    pipeline(blocks, forward_x, forward_y, mixed, inverse_x, inverse_y)
+    return out
 
 
 def lane_mask(shape, core):
@@ -143,8 +177,8 @@
     section = right(split(k_ref[...]), right_ref[...])
     for k in range(count):
         high, low = split(section[k * rows : (k + 1) * rows])
-        p_ref[k] = left(cos_ref[...], (high[:, :N], low[:, :N]))
-        q_ref[k] = left(sin_ref[...], (high[:, N:], low[:, N:]))
+        p_ref[k] = left(cos_ref[...], (high[:, :H], low[:, :H]))
+        q_ref[k] = left(sin_ref[...], (high[:, H:], low[:, H:]))
 
 
 TABLES = ("fx", "fy", "fy_own", "ix", "iy", "iy_own")
@@ -152,7 +186,7 @@
 
 def first_kernel(tiles, own_ref, s1_ref, r1_ref, s2_ref, r2_ref, p_ref, q_ref, *refs):
     t = dict(zip(TABLES, refs))
-    rest_ref, send_ref, target_ref, f_sc, a_sc, w_sc, z_sc = refs[len(TABLES) :]
+    rest_ref, send_ref, target_ref, f_sc, g_sc, x_sc, a_sc, w_sc, y_sc, u_sc, z_sc = refs[len(TABLES) :]
     core, tile, total = lax.axis_index("gy"), lax.axis_index("gx"), tiles * H
     count = p_ref.shape[0]
     low1 = jnp.where(core == 0, s1_ref[...], r1_ref[...])
@@ -164,10 +198,10 @@
     field = jnp.where(inside, field, 0.0)
     target = jnp.concatenate([low2[H:], low1[H:], own_ref[H:], upp1[H:], upp2[H:]], 0)
     target = jnp.where(core == 0, target[:, :H], target[:, H:])
-    amplitudes(4, field, p_ref, q_ref, t, f_sc, a_sc, core)
-    slopes(4 * H, count, a_sc, target, row_mask((4 * H, H), (tile - 1) * H - R, total), w_sc)
+    amplitudes(4, field, p_ref, q_ref, t, f_sc, g_sc, x_sc, a_sc, core)
+    slopes(4, count, a_sc, target, row_mask((4 * H, H), (tile - 1) * H - R, total), w_sc)
     target_ref[...] = target[H : 3 * H]
-    for b, part in enumerate(gradients(3, p_ref, q_ref, t, w_sc, z_sc, core)):
+    for b, part in enumerate(gradients(3, count, p_ref, q_ref, t, w_sc, y_sc, u_sc, z_sc, core)):
         rows = slice(b * H, (b + 1) * H)
         rest_ref[rows, :] = field[(b + 1) * H : (b + 2) * H] - STEP * part
         send_ref[rows, :] = pltpu.roll(part, N - R, 1)[:, :H]
@@ -175,18 +209,18 @@
 
 def second_kernel(tiles, rest_ref, got_ref, target_ref, p_ref, q_ref, *refs):
     t = dict(zip(TABLES, refs))
-    mask_ref, send_ref, resist_ref, f_sc, a_sc, w_sc, z_sc = refs[len(TABLES) :]
+    mask_ref, send_ref, resist_ref, f_sc, g_sc, x_sc, a_sc, w_sc, y_sc, u_sc, z_sc = refs[len(TABLES) :]
     core, tile, total = lax.axis_index("gy"), lax.axis_index("gx"), tiles * H
     count = p_ref.shape[0]
     got = jnp.concatenate([got_ref[...], jnp.zeros_like(got_ref)], 1)
     field = rest_ref[...] - STEP * pltpu.roll(got, R, 1)
     inside = row_mask(field.shape, (tile - 1) * H, total) & lane_mask(field.shape, core)
     field = jnp.where(inside, field, 0.0)
-    amplitudes(2, field, p_ref, q_ref, t, f_sc, a_sc, core)
+    amplitudes(2, field, p_ref, q_ref, t, f_sc, g_sc, x_sc, a_sc, core)
     inside = row_mask((2 * H, H), tile * H - R, total)
-    resist = slopes(2 * H, count, a_sc, target_ref[...], inside, w_sc)
-    resist_ref[...] = resist[R : R + H]
-    (part,) = gradients(1, p_ref, q_ref, t, w_sc, z_sc, core)
+    resist = slopes(2, count, a_sc, target_ref[...], inside, w_sc)
+    resist_ref[:R, :], resist_ref[R:, :] = resist[1], resist[2]
+    (part,) = gradients(1, count, p_ref, q_ref, t, w_sc, y_sc, u_sc, z_sc, core)
     part = jnp.where(lane_mask(part.shape, core), STEP * part, 0.0)
     own = field[H : 2 * H] - part
     mask_ref[...] = jnp.where(core == 0, own[:, :H], own[:, H:])
@@ -198,11 +232,16 @@
 
 
 def scratch(blocks, adjoint_blocks, count):
+    items = count * blocks
     return [
         pltpu.VMEM((blocks, N, N), jnp.float32),
+        pltpu.VMEM((items, 2, N, N), jnp.bfloat16),
+        pltpu.VMEM((2, items, H, N), jnp.bfloat16),
         pltpu.VMEM((count, blocks * H, H), jnp.float32),
-        pltpu.VMEM((count, blocks * H, N), jnp.bfloat16),
-        pltpu.VMEM((adjoint_blocks, N, N), jnp.float32),
+        pltpu.VMEM((2, blocks * H, count * H), jnp.bfloat16),
+        pltpu.VMEM((2, adjoint_blocks, N, count * H), jnp.bfloat16),
+        pltpu.VMEM((adjoint_blocks, count, N, N), jnp.float32),
+        pltpu.VMEM((adjoint_blocks, 2, N, N), jnp.bfloat16),
     ]
 
 
@@ -229,7 +268,7 @@
     spectral = [jnp.asarray(v) for v in spectral]
     p, q = pl.pallas_call(
         spectrum_kernel,
-        out_shape=(shape(count, N, N), shape(count, H, H)),
+        out_shape=(shape(count, H, H), shape(count, H, H)),
         in_specs=[VMEM] * 4,
         out_specs=(VMEM, VMEM),
         cost_estimate=pl.CostEstimate(
@@ -244,7 +283,7 @@
     tables = [
         stack(forward, 1),
         stack(forward.T, 0),
-        np.stack([np.roll(stack(forward.T[c], 0), H, 0) for c in halves]),
+        np.stack([stack(forward.T[c], 0) for c in halves]),
         stack(inverse[R : R + H], 1),
         stack(inverse.T, 0),
         np.stack([stack(inverse.T[:, c], 0) for c in halves]),

time: 37.5 us -> 33.8 us (0.901)
  Pallas kernels: 16.1 us -> 13.2 us
  other arithmetic: 3.35 us -> 1.57 us
  local copies, waits for them, and re-layouts: 0.29 us -> 1.56 us
    pallas_call x1, Pallas kernels: 9.86 us -> 7.56 us  [per_device(): pl.pallas_call(functools.partial(first_kernel, tiles), out_shape=(shape(3...]
    unnamed x18 -> x20, local copies, waits for them, and re-layouts: 0.24 us -> 1.51 us
    select_n x1, other arithmetic: 0.94 us -> 0.02 us  [per_device(): jnp.where(core == 0, jnp.concatenate([mine, mate], 1), jnp.concatenate([m...]
    concatenate x1, other arithmetic: 0.85 us -> 0.01 us  [per_device(): mine = jnp.concatenate([mask_init, target_map.astype(jnp.float32)], 0)]
    pallas_call x1, Pallas kernels: 5.35 us -> 4.75 us  [per_device(): pl.pallas_call(functools.partial(second_kernel, tiles), out_shape=(shape(...]
  transfers between devices with their start and end apart: 7 -> 7, of which waited for: 5 -> 4; matrix products, arithmetic and copies ran while one was open for 0% -> 0% of each run, Pallas kernels for 2% -> 3%
where the time goes in v2:
time: 33.8 us; the launch traced here: 33.6 us
  Pallas kernels  13.2 us (39%)
  waiting for transfers between devices  10.6 us (31%)
  starting transfers between devices  5.81 us (17%)
  other arithmetic  1.57 us (5%)
  local copies, waits for them, and re-layouts  1.56 us (5%)
  between operations  0.78 us (2%)
    pallas_call x1, Pallas kernels, per_device(): pl.pallas_call(functools.partial(first_kernel, tiles), out_shape=(shape(3...  7.56 us
    ppermute x1, waiting for transfers between devices, per_device(): s1 = lax.ppermute(own, ('gx', 'gy'), ring(1))  7.1 us
    pallas_call x1, Pallas kernels, per_device(): pl.pallas_call(functools.partial(second_kernel, tiles), out_shape=(shape(...  4.75 us
    ppermute x1, starting transfers between devices, per_device(): s1 = lax.ppermute(own, ('gx', 'gy'), ring(1))  2.93 us
    ppermute x1, starting transfers between devices, per_device(): s2 = lax.ppermute(far, ('gx', 'gy'), ring(2))  1.63 us
    unnamed x20, local copies, waits for them, and re-layouts  1.51 us
    ppermute x1, waiting for transfers between devices, per_device(): got = lax.ppermute(send, 'gy', swap)  1.43 us
    ppermute x1, waiting for transfers between devices, per_device(): return (mask - lax.ppermute(send, 'gy', swap), resist)  1.11 us
  transfers between devices with their start and end apart: 7, of which 4 were waited for; matrix products, arithmetic and copies ran while one was open for 0% of the time, Pallas kernels for 3%

profile of v2, /device:TPU:0, one launch (start us, length us, event | category | flops | bytes accessed | tf_op | source)
XLA Modules:
  0.0 33.6 jit_solution(14240803825013849900)
XLA Ops:
  0.6 0.0 copy-start.9
  0.6 0.9 %convert_element_type.5 = f32[128,128]{1,0:T(8,128)S(1)} convert(s32[128,128]{1,0:T(8,128)} %param.13) | non-fusion elementwise | flops 16384 | bytes 131072 | tf_op jit(solution)/shard_map/convert_element_type | solution.py:293
  1.5 0.0 copy-done.9
  1.5 0.5 %collective-permute-start = (f32[256,128]{1,0:T(8,128)S(1)}, f32[256,128]{1,0:T(8,128)S(1)}, u32[]{:S(2)}, u32[]{:S(2)}) collective-permute-start(f32[256,128]{1,0:T(8,128)S(1)} %pad_maximum_fusion.1), channel_id=1, source_target_pairs={{0,1},{1,0},{2,3},{3,2},{4,5},{5,4},{6,7},{7,6},{8,9},{9,8},{10,11... | collective-permute-start | bytes 393224 | tf_op jit(solution)/shard_map/ppermute | solution.py:294
  2.1 1.0 %collective-permute-done = f32[256,128]{1,0:T(8,128)S(1)} collective-permute-done((f32[256,128]{1,0:T(8,128)S(1)}, f32[256,128]{1,0:T(8,128)S(1)}, u32[]{:S(2)}, u32[]{:S(2)}) %collective-permute-start) | collective-permute-done | bytes 131104 | tf_op jit(solution)/shard_map/ppermute | solution.py:294
  3.1 2.9 %collective-permute-start.1 = (f32[256,256]{1,0:T(8,128)S(1)}, f32[256,256]{1,0:T(8,128)S(1)}, u32[]{:S(2)}, u32[]{:S(2)}) collective-permute-start(f32[256,256]{1,0:T(8,128)S(1)} %maximum_select_fusion.own_ref), channel_id=1, source_target_pairs={{0,2},{2,4},{4,6},{6,8},{8,10},{10,12},{12,14},{14,15},{15,13},{13... | collective-permute-start | bytes 786440 | tf_op jit(solution)/shard_map/ppermute | solution.py:299
  6.0 0.0 slice-start
  6.1 1.6 %collective-permute-start.3 = (f32[192,256]{1,0:T(8,128)S(1)}, f32[192,256]{1,0:T(8,128)S(1)}, u32[]{:S(2)}, u32[]{:S(2)}) collective-permute-start(f32[192,256]{1,0:T(8,128)S(1)} %pad_maximum_fusion), channel_id=1, source_target_pairs={{0,4},{2,6},{4,8},{6,10},{8,12},{10,14},{12,15},{14,13},{15,11},{1... | collective-permute-start | bytes 589832 | tf_op jit(solution)/shard_map/ppermute | solution.py:300
  7.7 7.1 %collective-permute-done.1.s1_ref = f32[256,256]{1,0:T(8,128)S(1)} collective-permute-done((f32[256,256]{1,0:T(8,128)S(1)}, f32[256,256]{1,0:T(8,128)S(1)}, u32[]{:S(2)}, u32[]{:S(2)}) %collective-permute-start.1) | collective-permute-done | bytes 262176 | tf_op jit(solution)/shard_map/ppermute | solution.py:299
  14.8 0.0 collective-permute-start.2
  14.8 0.0 collective-permute-done.3.s2_ref
  14.8 0.5 %collective-permute-start.4 = (f32[192,256]{1,0:T(8,128)S(1)}, f32[192,256]{1,0:T(8,128)S(1)}, u32[]{:S(2)}, u32[]{:S(2)}) collective-permute-start(f32[192,256]{1,0:T(8,128)S(1)} %collective-permute-done.3.s2_ref), channel_id=1, source_target_pairs={{0,1},{1,0},{2,3},{3,2},{4,5},{5,4},{6,7},{7,6},{8,9},{9,8},{10,11... | collective-permute-start | bytes 589832 | tf_op jit(solution)/shard_map/ppermute | solution.py:302
  15.3 0.0 slice-done
  15.3 0.0 copy-start.6
  15.3 0.0 copy-start.7
  15.3 0.0 copy-start.8
  15.4 0.9 %copy-done.6 = bf16[768,256]{1,0:T(8,128)(2,1)S(1)} copy-done((bf16[768,256]{1,0:T(8,128)(2,1)S(1)}, bf16[768,256]{1,0:T(8,128)(2,1)}, u32[]{:S(2)}) %copy-start.6) | copy-done | bytes 393240
  16.3 0.0 copy-done.7
  16.3 0.0 copy-done.8
  16.3 0.0 copy-start
  16.3 0.0 copy-start.1
  16.3 0.0 copy-start.2
  16.3 0.0 copy-start.3
  16.4 0.0 copy-start.4
  16.4 0.0 copy-start.5
  16.4 0.9 %spectra.1 = (f32[6,128,128]{2,1,0:T(8,128)S(1)}, f32[6,128,128]{2,1,0:T(8,128)S(1)}) custom-call(f32[432,256]{1,0:T(8,128)S(1)} %bitcast.1, bf16[768,256]{1,0:T(8,128)(2,1)S(1)} %copy-done.6, bf16[128,216]{1,0:T(8,128)(2,1)S(1)} %copy-done.8, bf16[128,216]{1,0:T(8,128)(2,1)S(1)} %copy-done.7), custom_call_target="tpu_custom_call" | custom-call | flops 679477248 | bytes 1572864 | tf_op jit(solution)/shard_map/spectra/pallas_call | solution.py:269
  17.3 0.0 collective-permute-done.4.r2_ref
  17.3 0.0 collective-permute-done.2.r1_ref
  17.3 0.0 copy-done
  17.3 0.1 copy-done.1
  17.4 0.1 copy-done.2
  17.6 0.1 copy-done.3
  17.7 0.1 copy-done.4
  17.8 0.0 copy-done.5
  17.8 7.6 %first_step.1 = (f32[384,256]{1,0:T(8,128)S(1)}, f32[384,128]{1,0:T(8,128)S(1)}, f32[256,128]{1,0:T(8,128)S(1)}) custom-call(f32[256,256]{1,0:T(8,128)S(1)} %maximum_select_fusion.own_ref, f32[256,256]{1,0:T(8,128)S(1)} %collective-permute-done.1.s1_ref, f32[256,256]{1,0:T(8,128)S(1)} %collective-permute-done.2.r1_ref, ...), custom_call_target="tpu_custom_call" | custom-call | tf_op jit(solution)/shard_map/first_step/pallas_call | solution.py:305
  25.4 0.1 collective-permute-start.5
  25.5 1.4 %collective-permute-done.5.got_ref = f32[384,128]{1,0:T(8,128)S(1)} collective-permute-done((f32[384,128]{1,0:T(8,128)S(1)}, f32[384,128]{1,0:T(8,128)S(1)}, u32[]{:S(2)}, u32[]{:S(2)}) %collective-permute-start.5) | collective-permute-done | bytes 196640 | tf_op jit(solution)/shard_map/ppermute | solution.py:314
  26.9 4.8 %second_step.1 = (f32[128,128]{1,0:T(8,128)S(1)}, f32[128,128]{1,0:T(8,128)S(1)}, f32[128,128]{1,0:T(8,128)}) custom-call(f32[384,256]{1,0:T(8,128)S(1)} %get-tuple-element.12.rest_ref, f32[384,128]{1,0:T(8,128)S(1)} %collective-permute-done.5.got_ref, f32[256,128]{1,0:T(8,128)S(1)} %get-tuple-element.14.target_ref, ...), custom_call_target="tpu_custom_call" | custom-call | tf_op jit(solution)/shard_map/second_step/pallas_call | solution.py:315
  31.7 0.1 collective-permute-start.6
  31.8 1.1 %collective-permute-done.6 = f32[128,128]{1,0:T(8,128)S(1)} collective-permute-done((f32[128,128]{1,0:T(8,128)S(1)}, f32[128,128]{1,0:T(8,128)S(1)}, u32[]{:S(2)}, u32[]{:S(2)}) %collective-permute-start.6) | collective-permute-done | bytes 65568 | tf_op jit(solution)/shard_map/ppermute | solution.py:324
  32.9 0.6 %sub.3 = f32[128,128]{1,0:T(8,128)} subtract(f32[128,128]{1,0:T(8,128)S(1)} %get-tuple-element.15, f32[128,128]{1,0:T(8,128)S(1)} %collective-permute-done.6) | non-fusion elementwise | flops 16384 | bytes 196608 | tf_op jit(solution)/shard_map/sub | solution.py:324
  (6 shorter events, 0.1 us)
Async XLA Ops:
  0.6 0.9 %copy-start.9 = (f32[128,128]{1,0:T(8,128)S(1)}, f32[128,128]{1,0:T(8,128)}, u32[]{:S(2)}) copy-start(f32[128,128]{1,0:T(8,128)} %param.12) | copy-start | bytes 196612
  1.5 1.5 %collective-permute-start = (f32[256,128]{1,0:T(8,128)S(1)}, f32[256,128]{1,0:T(8,128)S(1)}, u32[]{:S(2)}, u32[]{:S(2)}) collective-permute-start(f32[256,128]{1,0:T(8,128)S(1)} %pad_maximum_fusion.1), channel_id=1, source_target_pairs={{0,1},{1,0},{2,3},{3,2},{4,5},{5,4},{6,7},{7,6},{8,9},{9,8},{10,11... | collective-permute-start | bytes 393224 | tf_op jit(solution)/shard_map/ppermute | solution.py:294
  3.1 11.7 %collective-permute-start.1 = (f32[256,256]{1,0:T(8,128)S(1)}, f32[256,256]{1,0:T(8,128)S(1)}, u32[]{:S(2)}, u32[]{:S(2)}) collective-permute-start(f32[256,256]{1,0:T(8,128)S(1)} %maximum_select_fusion.own_ref), channel_id=1, source_target_pairs={{0,2},{2,4},{4,6},{6,8},{8,10},{10,12},{12,14},{14,15},{15,13},{13... | collective-permute-start | bytes 786440 | tf_op jit(solution)/shard_map/ppermute | solution.py:299
  6.0 9.3 %slice-start = ((f32[6,129,129]{2,1,0:T(8,128)}), f32[6,65,129]{2,1,0:T(8,128)S(1)}, s32[]{:S(2)}) async-start(f32[6,129,129]{2,1,0:T(8,128)} %param.14), calls=%async_computation | async-start | bytes 884736 | tf_op jit(solution)/shard_map/slice | solution.py:263
  6.1 8.7 %collective-permute-start.3 = (f32[192,256]{1,0:T(8,128)S(1)}, f32[192,256]{1,0:T(8,128)S(1)}, u32[]{:S(2)}, u32[]{:S(2)}) collective-permute-start(f32[192,256]{1,0:T(8,128)S(1)} %pad_maximum_fusion), channel_id=1, source_target_pairs={{0,4},{2,6},{4,8},{6,10},{8,12},{10,14},{12,15},{14,13},{15,11},{1... | collective-permute-start | bytes 589832 | tf_op jit(solution)/shard_map/ppermute | solution.py:300
  14.8 2.5 %collective-permute-start.2 = (f32[256,256]{1,0:T(8,128)S(1)}, f32[256,256]{1,0:T(8,128)S(1)}, u32[]{:S(2)}, u32[]{:S(2)}) collective-permute-start(f32[256,256]{1,0:T(8,128)S(1)} %collective-permute-done.1.s1_ref), channel_id=1, source_target_pairs={{0,1},{1,0},{2,3},{3,2},{4,5},{5,4},{6,7},{7,6},{8,9},{9,8},{10,11... | collective-permute-start | bytes 786440 | tf_op jit(solution)/shard_map/ppermute | solution.py:301
  14.8 2.5 %collective-permute-start.4 = (f32[192,256]{1,0:T(8,128)S(1)}, f32[192,256]{1,0:T(8,128)S(1)}, u32[]{:S(2)}, u32[]{:S(2)}) collective-permute-start(f32[192,256]{1,0:T(8,128)S(1)} %collective-permute-done.3.s2_ref), channel_id=1, source_target_pairs={{0,1},{1,0},{2,3},{3,2},{4,5},{5,4},{6,7},{7,6},{8,9},{9,8},{10,11... | collective-permute-start | bytes 589832 | tf_op jit(solution)/shard_map/ppermute | solution.py:302
  15.3 1.0 %copy-start.6 = (bf16[768,256]{1,0:T(8,128)(2,1)S(1)}, bf16[768,256]{1,0:T(8,128)(2,1)}, u32[]{:S(2)}) copy-start(bf16[768,256]{1,0:T(8,128)(2,1)} %constant.26.clone.right_ref) | copy-start | bytes 1179652
  15.3 1.0 %copy-start.7 = (bf16[128,216]{1,0:T(8,128)(2,1)S(1)}, bf16[128,216]{1,0:T(8,128)(2,1)}, u32[]{:S(2)}) copy-start(bf16[128,216]{1,0:T(8,128)(2,1)} %constant.28.clone.sin_ref) | copy-start | bytes 165892
  15.3 1.0 %copy-start.8 = (bf16[128,216]{1,0:T(8,128)(2,1)S(1)}, bf16[128,216]{1,0:T(8,128)(2,1)}, u32[]{:S(2)}) copy-start(bf16[128,216]{1,0:T(8,128)(2,1)} %constant.27.clone.cos_ref) | copy-start | bytes 165892
  16.3 1.0 %copy-start = (bf16[2,768,128]{2,1,0:T(8,128)(2,1)S(1)}, bf16[2,768,128]{2,1,0:T(8,128)(2,1)}, u32[]{:S(2)}) copy-start(bf16[2,768,128]{2,1,0:T(8,128)(2,1)} %constant.34.clone.refs_5_) | copy-start | bytes 1179652
  16.3 1.1 %copy-start.1 = (bf16[768,256]{1,0:T(8,128)(2,1)S(1)}, bf16[768,256]{1,0:T(8,128)(2,1)}, u32[]{:S(2)}) copy-start(bf16[768,256]{1,0:T(8,128)(2,1)} %constant.33.clone.refs_4_) | copy-start | bytes 1179652
  16.3 1.2 %copy-start.2 = (bf16[2,384,256]{2,1,0:T(8,128)(2,1)S(1)}, bf16[2,384,256]{2,1,0:T(8,128)(2,1)}, u32[]{:S(2)}) copy-start(bf16[2,384,256]{2,1,0:T(8,128)(2,1)} %constant.31.clone.refs_2_) | copy-start | bytes 1179652
  16.3 1.3 %copy-start.3 = (bf16[768,256]{1,0:T(8,128)(2,1)S(1)}, bf16[768,256]{1,0:T(8,128)(2,1)}, u32[]{:S(2)}) copy-start(bf16[768,256]{1,0:T(8,128)(2,1)} %constant.30.clone.refs_1_) | copy-start | bytes 1179652
  16.4 1.4 %copy-start.4 = (bf16[256,768]{1,0:T(8,128)(2,1)S(1)}, bf16[256,768]{1,0:T(8,128)(2,1)}, u32[]{:S(2)}) copy-start(bf16[256,768]{1,0:T(8,128)(2,1)} %constant.29.clone.refs_0_) | copy-start | bytes 1179652
  16.4 1.5 %copy-start.5 = (bf16[128,768]{1,0:T(8,128)(2,1)S(1)}, bf16[128,768]{1,0:T(8,128)(2,1)}, u32[]{:S(2)}) copy-start(bf16[128,768]{1,0:T(8,128)(2,1)} %constant.32.clone.refs_3_) | copy-start | bytes 589828
  25.4 1.5 %collective-permute-start.5 = (f32[384,128]{1,0:T(8,128)S(1)}, f32[384,128]{1,0:T(8,128)S(1)}, u32[]{:S(2)}, u32[]{:S(2)}) collective-permute-start(f32[384,128]{1,0:T(8,128)S(1)} %get-tuple-element.13), channel_id=1, source_target_pairs={{0,1},{1,0},{2,3},{3,2},{4,5},{5,4},{6,7},{7,6},{8,9},{9,8},{10,11... | collective-permute-start | bytes 589832 | tf_op jit(solution)/shard_map/ppermute | solution.py:314
  31.7 1.3 %collective-permute-start.6 = (f32[128,128]{1,0:T(8,128)S(1)}, f32[128,128]{1,0:T(8,128)S(1)}, u32[]{:S(2)}, u32[]{:S(2)}) collective-permute-start(f32[128,128]{1,0:T(8,128)S(1)} %get-tuple-element.16), channel_id=1, source_target_pairs={{0,1},{1,0},{2,3},{3,2},{4,5},{5,4},{6,7},{7,6},{8,9},{9,8},{10,11... | collective-permute-start | bytes 196616 | tf_op jit(solution)/shard_map/ppermute | solution.py:324

commit v3 on v2

--- a/solution.py
+++ b/solution.py
@@ -184,20 +184,24 @@
 TABLES = ("fx", "fy", "fy_own", "ix", "iy", "iy_own")
 
 
-def first_kernel(tiles, own_ref, s1_ref, r1_ref, s2_ref, r2_ref, p_ref, q_ref, *refs):
+def first_kernel(tiles, near_ref, a1_ref, b1_ref, a2_ref, b2_ref, mate_ref, p_ref, q_ref, *refs):
     t = dict(zip(TABLES, refs))
     rest_ref, send_ref, target_ref, f_sc, g_sc, x_sc, a_sc, w_sc, y_sc, u_sc, z_sc = refs[len(TABLES) :]
     core, tile, total = lax.axis_index("gy"), lax.axis_index("gx"), tiles * H
     count = p_ref.shape[0]
-    low1 = jnp.where(core == 0, s1_ref[...], r1_ref[...])
-    upp1 = jnp.where(core == 0, r1_ref[...], s1_ref[...])
-    low2 = jnp.where(core == 0, s2_ref[...], r2_ref[...])
-    upp2 = jnp.where(core == 0, r2_ref[...], s2_ref[...])
-    field = jnp.concatenate([low2[:H], low1[:H], own_ref[:H], upp1[:H], upp2[:H]], 0)
+    first = core == 0
+
+    def ordered(*parts):
+        pairs = zip(parts, parts[::-1])
+        return jnp.concatenate([jnp.where(first, x, y) for x, y in pairs], 0)
+
+    field = ordered(a2_ref[:H], a1_ref[:H], near_ref[:H], b1_ref[:H], b2_ref[:H])
+    mate = [mate_ref[c * H : (c + 1) * H] for c in range(5)]
+    mate = ordered(*mate[::-1])
+    field = jnp.concatenate([jnp.where(first, field, mate), jnp.where(first, mate, field)], 1)
     inside = row_mask(field.shape, (tile - 2) * H, total) & lane_mask(field.shape, core)
     field = jnp.where(inside, field, 0.0)
-    target = jnp.concatenate([low2[H:], low1[H:], own_ref[H:], upp1[H:], upp2[H:]], 0)
-    target = jnp.where(core == 0, target[:, :H], target[:, H:])
+    target = ordered(a2_ref[H:], a1_ref[H:], near_ref[H:], b1_ref[H:], b2_ref[H:])
     amplitudes(4, field, p_ref, q_ref, t, f_sc, g_sc, x_sc, a_sc, core)
     slopes(4, count, a_sc, target, row_mask((4 * H, H), (tile - 1) * H - R, total), w_sc)
     target_ref[...] = target[H : 3 * H]
@@ -290,27 +294,33 @@
     ]
     tables = [jnp.asarray(v) for v in tables]
 
-    mine = jnp.concatenate([mask_init, target_map.astype(jnp.float32)], 0)
-    mate = lax.ppermute(mine, "gy", swap)
-    own = jnp.where(
-        core == 0, jnp.concatenate([mine, mate], 1), jnp.concatenate([mate, mine], 1)
+    near = jnp.concatenate([mask_init, target_map.astype(jnp.float32)], 0)
+    first, second = near[H : H + R], near[H + R :]
+    up = jnp.concatenate([near[:H], jnp.where(core == 0, second, first)], 0)
+    down = jnp.concatenate([near[:H], jnp.where(core == 0, first, second)], 0)
+    both = ("gx", "gy")
+    around = [
+        lax.ppermute(near, both, ring(1)),
+        lax.ppermute(near, both, ring(-1)),
+        lax.ppermute(up, both, ring(2)),
+        lax.ppermute(down, both, ring(-2)),
+    ]
+    *around, p, q = lax.optimization_barrier((*around, p, q))
+    a1, b1, a2, b2 = around
+    mate = lax.ppermute(
+        jnp.concatenate([a2[:H], a1[:H], near[:H], b1[:H], b2[:H]], 0), "gy", swap
     )
-    far = jnp.concatenate([own[:H], jnp.where(core == 0, own[H + R :], own[H : H + R])], 0)
-    s1 = lax.ppermute(own, ("gx", "gy"), ring(1))
-    s2 = lax.ppermute(far, ("gx", "gy"), ring(2))
-    r1 = lax.ppermute(s1, "gy", swap)
-    r2 = lax.ppermute(s2, "gy", swap)
 
     params = pltpu.CompilerParams(vmem_limit_bytes=40 << 20)
     rest, send, target = pl.pallas_call(
         functools.partial(first_kernel, tiles),
         out_shape=(shape(3 * H, N), shape(3 * H, H), shape(2 * H, H)),
-        in_specs=[VMEM] * (7 + len(tables)),
+        in_specs=[VMEM] * (8 + len(tables)),
         out_specs=(VMEM,) * 3,
         scratch_shapes=scratch(4, 3, count),
         compiler_params=params,
         name="first_step",
-    )(own, s1, r1, s2, r2, p, q, *tables)
+    )(near, a1, b1, a2, b2, mate, p, q, *tables)
     got = lax.ppermute(send, "gy", swap)
     mask, send, resist = pl.pallas_call(
         functools.partial(second_kernel, tiles),

time: 33.8 us -> 30.7 us (0.908)
  the two profiles are of different devices: /device:TPU:0 before, /device:TPU:25 now
where the time goes in v3:
time: 30.7 us; the launch traced here: 30.5 us
  Pallas kernels  13.2 us (43%)
  waiting for transfers between devices  8.68 us (28%)
  starting transfers between devices  5.22 us (17%)
  other arithmetic  1.55 us (5%)
  local copies, waits for them, and re-layouts  1.07 us (3%)
  between operations  0.8 us (3%)
    pallas_call x1, Pallas kernels, per_device(): pl.pallas_call(functools.partial(first_kernel, tiles), out_shape=(shape(3...  7.54 us
    ppermute x1, waiting for transfers between devices, per_device(): lax.ppermute(up, both, ring(2))  5.11 us
    pallas_call x1, Pallas kernels, per_device(): pl.pallas_call(functools.partial(second_kernel, tiles), out_shape=(shape(...  4.76 us
    ppermute x1, starting transfers between devices, per_device(): lax.ppermute(up, both, ring(2))  1.44 us
    ppermute x1, starting transfers between devices, per_device(): lax.ppermute(near, both, ring(-1))  1.29 us
    ppermute x1, waiting for transfers between devices, per_device(): lax.ppermute(jnp.concatenate([a2[:H], a1[:H], near[:H], b1[:H], b2[:H]],...  1.26 us
    ppermute x1, starting transfers between devices, per_device(): lax.ppermute(near, both, ring(1))  1.13 us
    ppermute x1, waiting for transfers between devices, per_device(): got = lax.ppermute(send, 'gy', swap)  1.07 us
  transfers between devices with their start and end apart: 7, of which 5 were waited for; matrix products, arithmetic and copies ran while one was open for 0% of the time, Pallas kernels for 3%

profile of v3, /device:TPU:25, one launch (start us, length us, event | category | flops | bytes accessed | tf_op | source)
XLA Modules:
  0.0 30.5 jit_solution(5987875615203237657)
XLA Ops:
  0.6 0.0 copy-start.9
  0.6 0.9 %convert_element_type.5 = f32[128,128]{1,0:T(8,128)S(1)} convert(s32[128,128]{1,0:T(8,128)} %param.13) | non-fusion elementwise | flops 16384 | bytes 131072 | tf_op jit(solution)/shard_map/convert_element_type | solution.py:297
  1.5 0.0 copy-done.9
  1.5 1.3 %collective-permute-start.1 = (f32[256,128]{1,0:T(8,128)S(1)}, f32[256,128]{1,0:T(8,128)S(1)}, u32[]{:S(2)}, u32[]{:S(2)}) collective-permute-start(f32[256,128]{1,0:T(8,128)S(1)} %pad_maximum_fusion.near_ref), channel_id=1, source_target_pairs={{0,1},{2,0},{4,2},{6,4},{8,6},{10,8},{12,10},{14,12},{15,14},{13,1... | collective-permute-start | bytes 393224 | tf_op jit(solution)/shard_map/ppermute | solution.py:304
  2.8 1.1 %collective-permute-start = (f32[256,128]{1,0:T(8,128)S(1)}, f32[256,128]{1,0:T(8,128)S(1)}, u32[]{:S(2)}, u32[]{:S(2)}) collective-permute-start(f32[256,128]{1,0:T(8,128)S(1)} %pad_maximum_fusion.near_ref), channel_id=1, source_target_pairs={{0,2},{2,4},{4,6},{6,8},{8,10},{10,12},{12,14},{14,15},{15,13},{13... | collective-permute-start | bytes 393224 | tf_op jit(solution)/shard_map/ppermute | solution.py:303
  4.0 0.1 collective-permute-start.3
  4.1 0.0 slice-start
  4.1 1.4 %collective-permute-start.2 = (f32[192,128]{1,0:T(8,128)S(1)}, f32[192,128]{1,0:T(8,128)S(1)}, u32[]{:S(2)}, u32[]{:S(2)}) collective-permute-start(f32[192,128]{1,0:T(8,128)S(1)} %get-tuple-element.31), channel_id=1, source_target_pairs={{0,4},{2,6},{4,8},{6,10},{8,12},{10,14},{12,15},{14,13},{15,11},{1... | collective-permute-start | bytes 294920 | tf_op jit(solution)/shard_map/ppermute | solution.py:305
  5.5 0.0 slice-done
  5.5 0.0 copy-start.6
  5.5 0.0 copy-start.7
  5.5 0.0 copy-start.8
  5.6 0.9 %copy-done.6 = bf16[768,256]{1,0:T(8,128)(2,1)S(1)} copy-done((bf16[768,256]{1,0:T(8,128)(2,1)S(1)}, bf16[768,256]{1,0:T(8,128)(2,1)}, u32[]{:S(2)}) %copy-start.6) | copy-done | bytes 393240
  6.5 0.0 copy-done.7
  6.5 0.0 copy-done.8
  6.5 0.0 copy-start.1
  6.5 0.0 copy-start.2
  6.5 0.0 copy-start.3
  6.5 0.0 copy-start.4
  6.5 0.9 %spectra.1 = (f32[6,128,128]{2,1,0:T(8,128)S(1)}, f32[6,128,128]{2,1,0:T(8,128)S(1)}) custom-call(f32[432,256]{1,0:T(8,128)S(1)} %bitcast.1, bf16[768,256]{1,0:T(8,128)(2,1)S(1)} %copy-done.6, bf16[128,216]{1,0:T(8,128)(2,1)S(1)} %copy-done.8, bf16[128,216]{1,0:T(8,128)(2,1)S(1)} %copy-done.7), custom_call_target="tpu_custom_call" | custom-call | flops 679477248 | bytes 1572864 | tf_op jit(solution)/shard_map/spectra/pallas_call | solution.py:273
  7.5 0.0 copy-start
  7.5 0.3 %collective-permute-done.3.b2_ref = f32[192,128]{1,0:T(8,128)S(1)} collective-permute-done((f32[192,128]{1,0:T(8,128)S(1)}, f32[192,128]{1,0:T(8,128)S(1)}, u32[]{:S(2)}, u32[]{:S(2)}) %collective-permute-start.3) | collective-permute-done | bytes 98336 | tf_op jit(solution)/shard_map/ppermute | solution.py:306
  7.8 5.1 %collective-permute-done.2.a2_ref = f32[192,128]{1,0:T(8,128)S(1)} collective-permute-done((f32[192,128]{1,0:T(8,128)S(1)}, f32[192,128]{1,0:T(8,128)S(1)}, u32[]{:S(2)}, u32[]{:S(2)}) %collective-permute-start.2) | collective-permute-done | bytes 98336 | tf_op jit(solution)/shard_map/ppermute | solution.py:305
  12.9 0.0 collective-permute-done.1.b1_ref
  12.9 0.0 collective-permute-done.a1_ref
  12.9 0.0 copy-start.5
  13.0 0.5 %collective-permute-start.4 = (f32[640,128]{1,0:T(8,128)S(1)}, f32[640,128]{1,0:T(8,128)S(1)}, u32[]{:S(2)}, u32[]{:S(2)}) collective-permute-start(f32[640,128]{1,0:T(8,128)S(1)} %slice_dynamic-update-slice_fusion), channel_id=1, source_target_pairs={{0,1},{1,0},{2,3},{3,2},{4,5},{5,4},{6,7},{7,6},{8,9},{9,8},{10,11... | collective-permute-start | bytes 983048 | tf_op jit(solution)/shard_map/ppermute | solution.py:310
  13.5 1.3 %collective-permute-done.4.mate_ref = f32[640,128]{1,0:T(8,128)S(1)} collective-permute-done((f32[640,128]{1,0:T(8,128)S(1)}, f32[640,128]{1,0:T(8,128)S(1)}, u32[]{:S(2)}, u32[]{:S(2)}) %collective-permute-start.4) | collective-permute-done | bytes 327712 | tf_op jit(solution)/shard_map/ppermute | solution.py:310
  14.7 0.0 copy-done.1
  14.7 0.0 copy-done.2
  14.7 0.0 copy-done.3
  14.7 0.0 copy-done.4
  14.8 0.0 copy-done
  14.8 0.0 copy-done.5
  14.8 7.5 %first_step.1 = (f32[384,256]{1,0:T(8,128)S(1)}, f32[384,128]{1,0:T(8,128)S(1)}, f32[256,128]{1,0:T(8,128)S(1)}) custom-call(f32[256,128]{1,0:T(8,128)S(1)} %pad_maximum_fusion.near_ref, f32[256,128]{1,0:T(8,128)S(1)} %collective-permute-done.a1_ref, f32[256,128]{1,0:T(8,128)S(1)} %collective-permute-done.1.b1_ref, ...), custom_call_target="tpu_custom_call" | custom-call | tf_op jit(solution)/shard_map/first_step/pallas_call | solution.py:315
  22.3 0.4 %collective-permute-start.5 = (f32[384,128]{1,0:T(8,128)S(1)}, f32[384,128]{1,0:T(8,128)S(1)}, u32[]{:S(2)}, u32[]{:S(2)}) collective-permute-start(f32[384,128]{1,0:T(8,128)S(1)} %get-tuple-element.25), channel_id=1, source_target_pairs={{0,1},{1,0},{2,3},{3,2},{4,5},{5,4},{6,7},{7,6},{8,9},{9,8},{10,11... | collective-permute-start | bytes 589832 | tf_op jit(solution)/shard_map/ppermute | solution.py:324
  22.8 1.1 %collective-permute-done.5.got_ref = f32[384,128]{1,0:T(8,128)S(1)} collective-permute-done((f32[384,128]{1,0:T(8,128)S(1)}, f32[384,128]{1,0:T(8,128)S(1)}, u32[]{:S(2)}, u32[]{:S(2)}) %collective-permute-start.5) | collective-permute-done | bytes 196640 | tf_op jit(solution)/shard_map/ppermute | solution.py:324
  23.8 4.8 %second_step.1 = (f32[128,128]{1,0:T(8,128)S(1)}, f32[128,128]{1,0:T(8,128)S(1)}, f32[128,128]{1,0:T(8,128)}) custom-call(f32[384,256]{1,0:T(8,128)S(1)} %get-tuple-element.24.rest_ref, f32[384,128]{1,0:T(8,128)S(1)} %collective-permute-done.5.got_ref, f32[256,128]{1,0:T(8,128)S(1)} %get-tuple-element.26.target_ref, ...), custom_call_target="tpu_custom_call" | custom-call | tf_op jit(solution)/shard_map/second_step/pallas_call | solution.py:325
  28.6 0.4 %collective-permute-start.6 = (f32[128,128]{1,0:T(8,128)S(1)}, f32[128,128]{1,0:T(8,128)S(1)}, u32[]{:S(2)}, u32[]{:S(2)}) collective-permute-start(f32[128,128]{1,0:T(8,128)S(1)} %get-tuple-element.28), channel_id=1, source_target_pairs={{0,1},{1,0},{2,3},{3,2},{4,5},{5,4},{6,7},{7,6},{8,9},{9,8},{10,11... | collective-permute-start | bytes 196616 | tf_op jit(solution)/shard_map/ppermute | solution.py:334
  29.0 0.9 %collective-permute-done.6 = f32[128,128]{1,0:T(8,128)S(1)} collective-permute-done((f32[128,128]{1,0:T(8,128)S(1)}, f32[128,128]{1,0:T(8,128)S(1)}, u32[]{:S(2)}, u32[]{:S(2)}) %collective-permute-start.6) | collective-permute-done | bytes 65568 | tf_op jit(solution)/shard_map/ppermute | solution.py:334
  29.9 0.6 %sub.3 = f32[128,128]{1,0:T(8,128)} subtract(f32[128,128]{1,0:T(8,128)S(1)} %get-tuple-element.27, f32[128,128]{1,0:T(8,128)S(1)} %collective-permute-done.6) | non-fusion elementwise | flops 16384 | bytes 196608 | tf_op jit(solution)/shard_map/sub | solution.py:334
  (9 shorter events, 0.1 us)
Async XLA Ops:
  0.6 0.9 %copy-start.9 = (f32[128,128]{1,0:T(8,128)S(1)}, f32[128,128]{1,0:T(8,128)}, u32[]{:S(2)}) copy-start(f32[128,128]{1,0:T(8,128)} %param.12) | copy-start | bytes 196612
  1.5 11.4 %collective-permute-start.1 = (f32[256,128]{1,0:T(8,128)S(1)}, f32[256,128]{1,0:T(8,128)S(1)}, u32[]{:S(2)}, u32[]{:S(2)}) collective-permute-start(f32[256,128]{1,0:T(8,128)S(1)} %pad_maximum_fusion.near_ref), channel_id=1, source_target_pairs={{0,1},{2,0},{4,2},{6,4},{8,6},{10,8},{12,10},{14,12},{15,14},{13,1... | collective-permute-start | bytes 393224 | tf_op jit(solution)/shard_map/ppermute | solution.py:304
  2.8 10.1 %collective-permute-start = (f32[256,128]{1,0:T(8,128)S(1)}, f32[256,128]{1,0:T(8,128)S(1)}, u32[]{:S(2)}, u32[]{:S(2)}) collective-permute-start(f32[256,128]{1,0:T(8,128)S(1)} %pad_maximum_fusion.near_ref), channel_id=1, source_target_pairs={{0,2},{2,4},{4,6},{6,8},{8,10},{10,12},{12,14},{14,15},{15,13},{13... | collective-permute-start | bytes 393224 | tf_op jit(solution)/shard_map/ppermute | solution.py:303
  4.0 3.8 %collective-permute-start.3 = (f32[192,128]{1,0:T(8,128)S(1)}, f32[192,128]{1,0:T(8,128)S(1)}, u32[]{:S(2)}, u32[]{:S(2)}) collective-permute-start(f32[192,128]{1,0:T(8,128)S(1)} %get-tuple-element.30), channel_id=1, source_target_pairs={{0,3},{2,1},{4,0},{6,2},{8,4},{10,6},{12,8},{14,10},{15,12},{13,14... | collective-permute-start | bytes 294920 | tf_op jit(solution)/shard_map/ppermute | solution.py:306
  4.1 1.5 %slice-start = ((f32[6,129,129]{2,1,0:T(8,128)}), f32[6,65,129]{2,1,0:T(8,128)S(1)}, s32[]{:S(2)}) async-start(f32[6,129,129]{2,1,0:T(8,128)} %param.14), calls=%async_computation | async-start | bytes 884736 | tf_op jit(solution)/shard_map/slice | solution.py:267
  4.1 8.8 %collective-permute-start.2 = (f32[192,128]{1,0:T(8,128)S(1)}, f32[192,128]{1,0:T(8,128)S(1)}, u32[]{:S(2)}, u32[]{:S(2)}) collective-permute-start(f32[192,128]{1,0:T(8,128)S(1)} %get-tuple-element.31), channel_id=1, source_target_pairs={{0,4},{2,6},{4,8},{6,10},{8,12},{10,14},{12,15},{14,13},{15,11},{1... | collective-permute-start | bytes 294920 | tf_op jit(solution)/shard_map/ppermute | solution.py:305
  5.5 1.0 %copy-start.6 = (bf16[768,256]{1,0:T(8,128)(2,1)S(1)}, bf16[768,256]{1,0:T(8,128)(2,1)}, u32[]{:S(2)}) copy-start(bf16[768,256]{1,0:T(8,128)(2,1)} %constant.26.clone.right_ref) | copy-start | bytes 1179652
  5.5 1.0 %copy-start.7 = (bf16[128,216]{1,0:T(8,128)(2,1)S(1)}, bf16[128,216]{1,0:T(8,128)(2,1)}, u32[]{:S(2)}) copy-start(bf16[128,216]{1,0:T(8,128)(2,1)} %constant.28.clone.sin_ref) | copy-start | bytes 165892
  5.5 1.0 %copy-start.8 = (bf16[128,216]{1,0:T(8,128)(2,1)S(1)}, bf16[128,216]{1,0:T(8,128)(2,1)}, u32[]{:S(2)}) copy-start(bf16[128,216]{1,0:T(8,128)(2,1)} %constant.27.clone.cos_ref) | copy-start | bytes 165892
  6.5 8.2 %copy-start.1 = (bf16[768,256]{1,0:T(8,128)(2,1)S(1)}, bf16[768,256]{1,0:T(8,128)(2,1)}, u32[]{:S(2)}) copy-start(bf16[768,256]{1,0:T(8,128)(2,1)} %constant.33.clone.refs_4_) | copy-start | bytes 1179652
  6.5 8.2 %copy-start.2 = (bf16[2,384,256]{2,1,0:T(8,128)(2,1)S(1)}, bf16[2,384,256]{2,1,0:T(8,128)(2,1)}, u32[]{:S(2)}) copy-start(bf16[2,384,256]{2,1,0:T(8,128)(2,1)} %constant.31.clone.refs_2_) | copy-start | bytes 1179652
  6.5 8.2 %copy-start.3 = (bf16[768,256]{1,0:T(8,128)(2,1)S(1)}, bf16[768,256]{1,0:T(8,128)(2,1)}, u32[]{:S(2)}) copy-start(bf16[768,256]{1,0:T(8,128)(2,1)} %constant.30.clone.refs_1_) | copy-start | bytes 1179652
  6.5 8.2 %copy-start.4 = (bf16[256,768]{1,0:T(8,128)(2,1)S(1)}, bf16[256,768]{1,0:T(8,128)(2,1)}, u32[]{:S(2)}) copy-start(bf16[256,768]{1,0:T(8,128)(2,1)} %constant.29.clone.refs_0_) | copy-start | bytes 1179652
  7.5 7.3 %copy-start = (bf16[2,768,128]{2,1,0:T(8,128)(2,1)S(1)}, bf16[2,768,128]{2,1,0:T(8,128)(2,1)}, u32[]{:S(2)}) copy-start(bf16[2,768,128]{2,1,0:T(8,128)(2,1)} %constant.34.clone.refs_5_) | copy-start | bytes 1179652
  12.9 1.8 %copy-start.5 = (bf16[128,768]{1,0:T(8,128)(2,1)S(1)}, bf16[128,768]{1,0:T(8,128)(2,1)}, u32[]{:S(2)}) copy-start(bf16[128,768]{1,0:T(8,128)(2,1)} %constant.32.clone.refs_3_) | copy-start | bytes 589828
  13.0 1.7 %collective-permute-start.4 = (f32[640,128]{1,0:T(8,128)S(1)}, f32[640,128]{1,0:T(8,128)S(1)}, u32[]{:S(2)}, u32[]{:S(2)}) collective-permute-start(f32[640,128]{1,0:T(8,128)S(1)} %slice_dynamic-update-slice_fusion), channel_id=1, source_target_pairs={{0,1},{1,0},{2,3},{3,2},{4,5},{5,4},{6,7},{7,6},{8,9},{9,8},{10,11... | collective-permute-start | bytes 983048 | tf_op jit(solution)/shard_map/ppermute | solution.py:310
  22.3 1.5 %collective-permute-start.5 = (f32[384,128]{1,0:T(8,128)S(1)}, f32[384,128]{1,0:T(8,128)S(1)}, u32[]{:S(2)}, u32[]{:S(2)}) collective-permute-start(f32[384,128]{1,0:T(8,128)S(1)} %get-tuple-element.25), channel_id=1, source_target_pairs={{0,1},{1,0},{2,3},{3,2},{4,5},{5,4},{6,7},{7,6},{8,9},{9,8},{10,11... | collective-permute-start | bytes 589832 | tf_op jit(solution)/shard_map/ppermute | solution.py:324
  28.6 1.3 %collective-permute-start.6 = (f32[128,128]{1,0:T(8,128)S(1)}, f32[128,128]{1,0:T(8,128)S(1)}, u32[]{:S(2)}, u32[]{:S(2)}) collective-permute-start(f32[128,128]{1,0:T(8,128)S(1)} %get-tuple-element.28), channel_id=1, source_target_pairs={{0,1},{1,0},{2,3},{3,2},{4,5},{5,4},{6,7},{7,6},{8,9},{9,8},{10,11... | collective-permute-start | bytes 196616 | tf_op jit(solution)/shard_map/ppermute | solution.py:334

commit v4 on v3

--- a/solution.py
+++ b/solution.py
@@ -255,12 +255,12 @@
     tile = lax.axis_index("gx")
     swap = [(0, 1), (1, 0)]
 
-    def place(step):
-        step %= 2 * tiles
-        return 2 * step if step < tiles else 2 * (2 * tiles - 1 - step) + 1
-
     def ring(shift):
-        return [(place(i), place(i + shift)) for i in range(2 * tiles)]
+        pairs = []
+        for x in range(tiles):
+            for c, to in ((0, x + shift), (1, x - shift)):
+                pairs.append((2 * x + c, 2 * to + c if 0 <= to < tiles else 2 * x + 1 - c))
+        return pairs
 
     rows = 72
     half = jnp.pad(

time: 30.7 us -> 30.1 us (0.980)
  the two profiles are of different devices: /device:TPU:25 before, /device:TPU:0 now
where the time goes in v4:
time: 30.1 us; the launch traced here: 30 us
  Pallas kernels  13.2 us (44%)
  waiting for transfers between devices  7.67 us (25%)
  starting transfers between devices  5.65 us (19%)
  other arithmetic  1.55 us (5%)
  local copies, waits for them, and re-layouts  1.07 us (4%)
  between operations  0.81 us (3%)
    pallas_call x1, Pallas kernels, per_device(): pl.pallas_call(functools.partial(first_kernel, tiles), out_shape=(shape(3...  7.55 us
    pallas_call x1, Pallas kernels, per_device(): pl.pallas_call(functools.partial(second_kernel, tiles), out_shape=(shape(...  4.75 us
    ppermute x1, waiting for transfers between devices, per_device(): lax.ppermute(down, both, ring(-2))  3.72 us
    ppermute x1, starting transfers between devices, per_device(): lax.ppermute(near, both, ring(1))  2.58 us
    ppermute x1, starting transfers between devices, per_device(): lax.ppermute(up, both, ring(2))  2.03 us
    ppermute x1, waiting for transfers between devices, per_device(): lax.ppermute(jnp.concatenate([a2[:H], a1[:H], near[:H], b1[:H], b2[:H]],...  1.52 us
    ppermute x1, waiting for transfers between devices, per_device(): got = lax.ppermute(send, 'gy', swap)  1.31 us
    ppermute x1, waiting for transfers between devices, per_device(): return (mask - lax.ppermute(send, 'gy', swap), resist)  1.11 us
  transfers between devices with their start and end apart: 7, of which 4 were waited for; matrix products, arithmetic and copies ran while one was open for 0% of the time, Pallas kernels for 3%

profile of v4, /device:TPU:0, one launch (start us, length us, event | category | flops | bytes accessed | tf_op | source)
XLA Modules:
  0.0 30.0 jit_solution(7195322561223024451)
XLA Ops:
  0.6 0.0 copy-start.9
  0.6 0.9 %convert_element_type.5 = f32[128,128]{1,0:T(8,128)S(1)} convert(s32[128,128]{1,0:T(8,128)} %param.13) | non-fusion elementwise | flops 16384 | bytes 131072 | tf_op jit(solution)/shard_map/convert_element_type | solution.py:297
  1.5 0.0 copy-done.9
  1.5 0.5 %collective-permute-start.1 = (f32[256,128]{1,0:T(8,128)S(1)}, f32[256,128]{1,0:T(8,128)S(1)}, u32[]{:S(2)}, u32[]{:S(2)}) collective-permute-start(f32[256,128]{1,0:T(8,128)S(1)} %pad_maximum_fusion.near_ref), channel_id=1, source_target_pairs={{0,1},{1,3},{2,0},{3,5},{4,2},{5,7},{6,4},{7,9},{8,6},{9,11},{10,8... | collective-permute-start | bytes 393224 | tf_op jit(solution)/shard_map/ppermute | solution.py:304
  2.0 2.6 %collective-permute-start = (f32[256,128]{1,0:T(8,128)S(1)}, f32[256,128]{1,0:T(8,128)S(1)}, u32[]{:S(2)}, u32[]{:S(2)}) collective-permute-start(f32[256,128]{1,0:T(8,128)S(1)} %pad_maximum_fusion.near_ref), channel_id=1, source_target_pairs={{0,2},{1,0},{2,4},{3,1},{4,6},{5,3},{6,8},{7,5},{8,10},{9,7},{10,1... | collective-permute-start | bytes 393224 | tf_op jit(solution)/shard_map/ppermute | solution.py:303
  4.7 0.0 collective-permute-start.3
  4.7 0.0 slice-start
  4.7 2.0 %collective-permute-start.2 = (f32[192,128]{1,0:T(8,128)S(1)}, f32[192,128]{1,0:T(8,128)S(1)}, u32[]{:S(2)}, u32[]{:S(2)}) collective-permute-start(f32[192,128]{1,0:T(8,128)S(1)} %get-tuple-element.31), channel_id=1, source_target_pairs={{0,4},{1,0},{2,6},{3,2},{4,8},{5,1},{6,10},{7,3},{8,12},{9,5},{10,... | collective-permute-start | bytes 294920 | tf_op jit(solution)/shard_map/ppermute | solution.py:305
  6.7 0.0 slice-done
  6.7 0.0 copy-start.6
  6.7 0.0 copy-start.7
  6.7 0.0 copy-start.8
  6.8 0.9 %copy-done.6 = bf16[768,256]{1,0:T(8,128)(2,1)S(1)} copy-done((bf16[768,256]{1,0:T(8,128)(2,1)S(1)}, bf16[768,256]{1,0:T(8,128)(2,1)}, u32[]{:S(2)}) %copy-start.6) | copy-done | bytes 393240
  7.7 0.0 copy-done.7
  7.7 0.0 copy-done.8
  7.7 0.0 copy-start.1
  7.7 0.0 copy-start.2
  7.7 0.0 copy-start.3
  7.8 0.0 copy-start.4
  7.8 0.9 %spectra.1 = (f32[6,128,128]{2,1,0:T(8,128)S(1)}, f32[6,128,128]{2,1,0:T(8,128)S(1)}) custom-call(f32[432,256]{1,0:T(8,128)S(1)} %bitcast.1, bf16[768,256]{1,0:T(8,128)(2,1)S(1)} %copy-done.6, bf16[128,216]{1,0:T(8,128)(2,1)S(1)} %copy-done.8, bf16[128,216]{1,0:T(8,128)(2,1)S(1)} %copy-done.7), custom_call_target="tpu_custom_call" | custom-call | flops 679477248 | bytes 1572864 | tf_op jit(solution)/shard_map/spectra/pallas_call | solution.py:273
  8.7 0.0 copy-start
  8.7 3.7 %collective-permute-done.3.b2_ref = f32[192,128]{1,0:T(8,128)S(1)} collective-permute-done((f32[192,128]{1,0:T(8,128)S(1)}, f32[192,128]{1,0:T(8,128)S(1)}, u32[]{:S(2)}, u32[]{:S(2)}) %collective-permute-start.3) | collective-permute-done | bytes 98336 | tf_op jit(solution)/shard_map/ppermute | solution.py:306
  12.4 0.0 collective-permute-done.2.a2_ref
  12.4 0.0 collective-permute-done.1.b1_ref
  12.4 0.0 collective-permute-done.a1_ref
  12.4 0.0 copy-start.5
  12.5 0.2 collective-permute-start.4
  12.7 1.5 %collective-permute-done.4.mate_ref = f32[640,128]{1,0:T(8,128)S(1)} collective-permute-done((f32[640,128]{1,0:T(8,128)S(1)}, f32[640,128]{1,0:T(8,128)S(1)}, u32[]{:S(2)}, u32[]{:S(2)}) %collective-permute-start.4) | collective-permute-done | bytes 327712 | tf_op jit(solution)/shard_map/ppermute | solution.py:310
  14.2 0.0 copy-done.1
  14.2 0.0 copy-done.2
  14.2 0.0 copy-done.3
  14.2 0.0 copy-done.4
  14.2 0.0 copy-done
  14.2 0.0 copy-done.5
  14.2 7.5 %first_step.1 = (f32[384,256]{1,0:T(8,128)S(1)}, f32[384,128]{1,0:T(8,128)S(1)}, f32[256,128]{1,0:T(8,128)S(1)}) custom-call(f32[256,128]{1,0:T(8,128)S(1)} %pad_maximum_fusion.near_ref, f32[256,128]{1,0:T(8,128)S(1)} %collective-permute-done.a1_ref, f32[256,128]{1,0:T(8,128)S(1)} %collective-permute-done.1.b1_ref, ...), custom_call_target="tpu_custom_call" | custom-call | tf_op jit(solution)/shard_map/first_step/pallas_call | solution.py:315
  21.8 0.2 collective-permute-start.5
  22.0 1.3 %collective-permute-done.5.got_ref = f32[384,128]{1,0:T(8,128)S(1)} collective-permute-done((f32[384,128]{1,0:T(8,128)S(1)}, f32[384,128]{1,0:T(8,128)S(1)}, u32[]{:S(2)}, u32[]{:S(2)}) %collective-permute-start.5) | collective-permute-done | bytes 196640 | tf_op jit(solution)/shard_map/ppermute | solution.py:324
  23.3 4.8 %second_step.1 = (f32[128,128]{1,0:T(8,128)S(1)}, f32[128,128]{1,0:T(8,128)S(1)}, f32[128,128]{1,0:T(8,128)}) custom-call(f32[384,256]{1,0:T(8,128)S(1)} %get-tuple-element.24.rest_ref, f32[384,128]{1,0:T(8,128)S(1)} %collective-permute-done.5.got_ref, f32[256,128]{1,0:T(8,128)S(1)} %get-tuple-element.26.target_ref, ...), custom_call_target="tpu_custom_call" | custom-call | tf_op jit(solution)/shard_map/second_step/pallas_call | solution.py:325
  28.1 0.1 collective-permute-start.6
  28.2 1.1 %collective-permute-done.6 = f32[128,128]{1,0:T(8,128)S(1)} collective-permute-done((f32[128,128]{1,0:T(8,128)S(1)}, f32[128,128]{1,0:T(8,128)S(1)}, u32[]{:S(2)}, u32[]{:S(2)}) %collective-permute-start.6) | collective-permute-done | bytes 65568 | tf_op jit(solution)/shard_map/ppermute | solution.py:334
  29.3 0.6 %sub.3 = f32[128,128]{1,0:T(8,128)} subtract(f32[128,128]{1,0:T(8,128)S(1)} %get-tuple-element.27, f32[128,128]{1,0:T(8,128)S(1)} %collective-permute-done.6) | non-fusion elementwise | flops 16384 | bytes 196608 | tf_op jit(solution)/shard_map/sub | solution.py:334
  (9 shorter events, 0.1 us)
Async XLA Ops:
  0.6 0.9 %copy-start.9 = (f32[128,128]{1,0:T(8,128)S(1)}, f32[128,128]{1,0:T(8,128)}, u32[]{:S(2)}) copy-start(f32[128,128]{1,0:T(8,128)} %param.12) | copy-start | bytes 196612
  1.5 10.9 %collective-permute-start.1 = (f32[256,128]{1,0:T(8,128)S(1)}, f32[256,128]{1,0:T(8,128)S(1)}, u32[]{:S(2)}, u32[]{:S(2)}) collective-permute-start(f32[256,128]{1,0:T(8,128)S(1)} %pad_maximum_fusion.near_ref), channel_id=1, source_target_pairs={{0,1},{1,3},{2,0},{3,5},{4,2},{5,7},{6,4},{7,9},{8,6},{9,11},{10,8... | collective-permute-start | bytes 393224 | tf_op jit(solution)/shard_map/ppermute | solution.py:304
  2.0 10.4 %collective-permute-start = (f32[256,128]{1,0:T(8,128)S(1)}, f32[256,128]{1,0:T(8,128)S(1)}, u32[]{:S(2)}, u32[]{:S(2)}) collective-permute-start(f32[256,128]{1,0:T(8,128)S(1)} %pad_maximum_fusion.near_ref), channel_id=1, source_target_pairs={{0,2},{1,0},{2,4},{3,1},{4,6},{5,3},{6,8},{7,5},{8,10},{9,7},{10,1... | collective-permute-start | bytes 393224 | tf_op jit(solution)/shard_map/ppermute | solution.py:303
  4.7 7.8 %collective-permute-start.3 = (f32[192,128]{1,0:T(8,128)S(1)}, f32[192,128]{1,0:T(8,128)S(1)}, u32[]{:S(2)}, u32[]{:S(2)}) collective-permute-start(f32[192,128]{1,0:T(8,128)S(1)} %get-tuple-element.30), channel_id=1, source_target_pairs={{0,1},{1,5},{2,3},{3,7},{4,0},{5,9},{6,2},{7,11},{8,4},{9,13},{10,... | collective-permute-start | bytes 294920 | tf_op jit(solution)/shard_map/ppermute | solution.py:306
  4.7 2.0 %slice-start = ((f32[6,129,129]{2,1,0:T(8,128)}), f32[6,65,129]{2,1,0:T(8,128)S(1)}, s32[]{:S(2)}) async-start(f32[6,129,129]{2,1,0:T(8,128)} %param.14), calls=%async_computation | async-start | bytes 884736 | tf_op jit(solution)/shard_map/slice | solution.py:267
  4.7 7.7 %collective-permute-start.2 = (f32[192,128]{1,0:T(8,128)S(1)}, f32[192,128]{1,0:T(8,128)S(1)}, u32[]{:S(2)}, u32[]{:S(2)}) collective-permute-start(f32[192,128]{1,0:T(8,128)S(1)} %get-tuple-element.31), channel_id=1, source_target_pairs={{0,4},{1,0},{2,6},{3,2},{4,8},{5,1},{6,10},{7,3},{8,12},{9,5},{10,... | collective-permute-start | bytes 294920 | tf_op jit(solution)/shard_map/ppermute | solution.py:305
  6.7 1.0 %copy-start.6 = (bf16[768,256]{1,0:T(8,128)(2,1)S(1)}, bf16[768,256]{1,0:T(8,128)(2,1)}, u32[]{:S(2)}) copy-start(bf16[768,256]{1,0:T(8,128)(2,1)} %constant.26.clone.right_ref) | copy-start | bytes 1179652
  6.7 1.0 %copy-start.7 = (bf16[128,216]{1,0:T(8,128)(2,1)S(1)}, bf16[128,216]{1,0:T(8,128)(2,1)}, u32[]{:S(2)}) copy-start(bf16[128,216]{1,0:T(8,128)(2,1)} %constant.28.clone.sin_ref) | copy-start | bytes 165892
  6.7 1.0 %copy-start.8 = (bf16[128,216]{1,0:T(8,128)(2,1)S(1)}, bf16[128,216]{1,0:T(8,128)(2,1)}, u32[]{:S(2)}) copy-start(bf16[128,216]{1,0:T(8,128)(2,1)} %constant.27.clone.cos_ref) | copy-start | bytes 165892
  7.7 6.5 %copy-start.1 = (bf16[768,256]{1,0:T(8,128)(2,1)S(1)}, bf16[768,256]{1,0:T(8,128)(2,1)}, u32[]{:S(2)}) copy-start(bf16[768,256]{1,0:T(8,128)(2,1)} %constant.33.clone.refs_4_) | copy-start | bytes 1179652
  7.7 6.5 %copy-start.2 = (bf16[2,384,256]{2,1,0:T(8,128)(2,1)S(1)}, bf16[2,384,256]{2,1,0:T(8,128)(2,1)}, u32[]{:S(2)}) copy-start(bf16[2,384,256]{2,1,0:T(8,128)(2,1)} %constant.31.clone.refs_2_) | copy-start | bytes 1179652
  7.7 6.5 %copy-start.3 = (bf16[768,256]{1,0:T(8,128)(2,1)S(1)}, bf16[768,256]{1,0:T(8,128)(2,1)}, u32[]{:S(2)}) copy-start(bf16[768,256]{1,0:T(8,128)(2,1)} %constant.30.clone.refs_1_) | copy-start | bytes 1179652
  7.8 6.5 %copy-start.4 = (bf16[256,768]{1,0:T(8,128)(2,1)S(1)}, bf16[256,768]{1,0:T(8,128)(2,1)}, u32[]{:S(2)}) copy-start(bf16[256,768]{1,0:T(8,128)(2,1)} %constant.29.clone.refs_0_) | copy-start | bytes 1179652
  8.7 5.5 %copy-start = (bf16[2,768,128]{2,1,0:T(8,128)(2,1)S(1)}, bf16[2,768,128]{2,1,0:T(8,128)(2,1)}, u32[]{:S(2)}) copy-start(bf16[2,768,128]{2,1,0:T(8,128)(2,1)} %constant.34.clone.refs_5_) | copy-start | bytes 1179652
  12.4 1.8 %copy-start.5 = (bf16[128,768]{1,0:T(8,128)(2,1)S(1)}, bf16[128,768]{1,0:T(8,128)(2,1)}, u32[]{:S(2)}) copy-start(bf16[128,768]{1,0:T(8,128)(2,1)} %constant.32.clone.refs_3_) | copy-start | bytes 589828
  12.5 1.7 %collective-permute-start.4 = (f32[640,128]{1,0:T(8,128)S(1)}, f32[640,128]{1,0:T(8,128)S(1)}, u32[]{:S(2)}, u32[]{:S(2)}) collective-permute-start(f32[640,128]{1,0:T(8,128)S(1)} %slice_dynamic-update-slice_fusion), channel_id=1, source_target_pairs={{0,1},{1,0},{2,3},{3,2},{4,5},{5,4},{6,7},{7,6},{8,9},{9,8},{10,11... | collective-permute-start | bytes 983048 | tf_op jit(solution)/shard_map/ppermute | solution.py:310
  21.8 1.5 %collective-permute-start.5 = (f32[384,128]{1,0:T(8,128)S(1)}, f32[384,128]{1,0:T(8,128)S(1)}, u32[]{:S(2)}, u32[]{:S(2)}) collective-permute-start(f32[384,128]{1,0:T(8,128)S(1)} %get-tuple-element.25), channel_id=1, source_target_pairs={{0,1},{1,0},{2,3},{3,2},{4,5},{5,4},{6,7},{7,6},{8,9},{9,8},{10,11... | collective-permute-start | bytes 589832 | tf_op jit(solution)/shard_map/ppermute | solution.py:324
  28.1 1.3 %collective-permute-start.6 = (f32[128,128]{1,0:T(8,128)S(1)}, f32[128,128]{1,0:T(8,128)S(1)}, u32[]{:S(2)}, u32[]{:S(2)}) collective-permute-start(f32[128,128]{1,0:T(8,128)S(1)} %get-tuple-element.28), channel_id=1, source_target_pairs={{0,1},{1,0},{2,3},{3,2},{4,5},{5,4},{6,7},{7,6},{8,9},{9,8},{10,11... | collective-permute-start | bytes 196616 | tf_op jit(solution)/shard_map/ppermute | solution.py:334

commit v5 on v4

--- a/solution.py
+++ b/solution.py
@@ -85,21 +85,21 @@
 
 
 def pipeline(count, *stages):
-    for step in range(count + len(stages) - 1):
-        for lag, stage in enumerate(reversed(stages)):
-            item = step - (len(stages) - 1 - lag)
+    for step in range(count + 2 * (len(stages) - 1)):
+        for place, stage in enumerate(stages):
+            item = step - 2 * place
             if 0 <= item < count:
                 stage(item)
 
 
-def amplitudes(blocks, field, p_ref, q_ref, t, f_sc, g_sc, x_sc, a_sc, core):
+def amplitudes(blocks, count, field, p_ref, q_ref, t, f_sc, g_sc, x_sc, a_sc, core, ready):
     ey = split(right(split(field), t["fy"][...]))
     for b in range(blocks):
         rows = slice(b * H, b * H + N)
         f_sc[b] = left(t["fx"][...], (ey[0][rows], ey[1][rows]))
 
     def mixed(i):
-        k, b = i // blocks, i % blocks
+        b, k = i // count, i % count
         for rows in CHUNKS:
             quarters = mix(f_sc.at[b], p_ref.at[k], q_ref.at[k], rows)
             store_quarters(g_sc.at[i], rows, quarters)
@@ -109,15 +109,17 @@
         x_sc[0, i], x_sc[1, i] = split(x)
 
     def inverse_y(i):
-        k, b = i // blocks, i % blocks
+        b, k = i // count, i % count
         a_sc[k, b * H : (b + 1) * H, :] = right((x_sc[0, i], x_sc[1, i]), t["iy_own"][core])
-
-    pipeline(p_ref.shape[0] * blocks, mixed, inverse_x, inverse_y)
-
-
-def slopes(blocks, count, a_sc, target, inside, w_sc):
+        if k == count - 1:
+            ready(b)
+
+    pipeline(count * blocks, mixed, inverse_x, inverse_y)
+
+
+def slopes(b, count, a_sc, target, inside, w_sc):
     resists = []
-    for c in range(0, blocks * H, R):
+    for c in range(b * H, (b + 1) * H, R):
         rows = slice(c, c + R)
         amplitude = [a_sc[k, rows, :] for k in range(count)]
         total = amplitude[0] * amplitude[0]
@@ -202,8 +204,12 @@
     inside = row_mask(field.shape, (tile - 2) * H, total) & lane_mask(field.shape, core)
     field = jnp.where(inside, field, 0.0)
     target = ordered(a2_ref[H:], a1_ref[H:], near_ref[H:], b1_ref[H:], b2_ref[H:])
-    amplitudes(4, field, p_ref, q_ref, t, f_sc, g_sc, x_sc, a_sc, core)
-    slopes(4, count, a_sc, target, row_mask((4 * H, H), (tile - 1) * H - R, total), w_sc)
+    inside = row_mask((4 * H, H), (tile - 1) * H - R, total)
+
+    def ready(b):
+        slopes(b, count, a_sc, target, inside, w_sc)
+
+    amplitudes(4, count, field, p_ref, q_ref, t, f_sc, g_sc, x_sc, a_sc, core, ready)
     target_ref[...] = target[H : 3 * H]
     for b, part in enumerate(gradients(3, count, p_ref, q_ref, t, w_sc, y_sc, u_sc, z_sc, core)):
         rows = slice(b * H, (b + 1) * H)
@@ -220,10 +226,14 @@
     field = rest_ref[...] - STEP * pltpu.roll(got, R, 1)
     inside = row_mask(field.shape, (tile - 1) * H, total) & lane_mask(field.shape, core)
     field = jnp.where(inside, field, 0.0)
-    amplitudes(2, field, p_ref, q_ref, t, f_sc, g_sc, x_sc, a_sc, core)
     inside = row_mask((2 * H, H), tile * H - R, total)
-    resist = slopes(2, count, a_sc, target_ref[...], inside, w_sc)
-    resist_ref[:R, :], resist_ref[R:, :] = resist[1], resist[2]
+    target = target_ref[...]
+
+    def ready(b):
+        resist = slopes(b, count, a_sc, target, inside, w_sc)
+        resist_ref[b * R : (b + 1) * R, :] = resist[1 - b]
+
+    amplitudes(2, count, field, p_ref, q_ref, t, f_sc, g_sc, x_sc, a_sc, core, ready)
     (part,) = gradients(1, count, p_ref, q_ref, t, w_sc, y_sc, u_sc, z_sc, core)
     part = jnp.where(lane_mask(part.shape, core), STEP * part, 0.0)
     own = field[H : 2 * H] - part

time: 30.1 us -> 29.8 us (0.990)
  no operation moved by 1% of the time
where the time goes in v5:
time: 29.8 us; the launch traced here: 29.6 us
  Pallas kernels  12.9 us (43%)
  waiting for transfers between devices  7.68 us (26%)
  starting transfers between devices  5.65 us (19%)
  other arithmetic  1.55 us (5%)
  local copies, waits for them, and re-layouts  1.07 us (4%)
  between operations  0.81 us (3%)
    pallas_call x1, Pallas kernels, per_device(): pl.pallas_call(functools.partial(first_kernel, tiles), out_shape=(shape(3...  7.34 us
    pallas_call x1, Pallas kernels, per_device(): pl.pallas_call(functools.partial(second_kernel, tiles), out_shape=(shape(...  4.65 us
    ppermute x1, waiting for transfers between devices, per_device(): lax.ppermute(down, both, ring(-2))  3.72 us
    ppermute x1, starting transfers between devices, per_device(): lax.ppermute(near, both, ring(1))  2.58 us
    ppermute x1, starting transfers between devices, per_device(): lax.ppermute(up, both, ring(2))  2.03 us
    ppermute x1, waiting for transfers between devices, per_device(): lax.ppermute(jnp.concatenate([a2[:H], a1[:H], near[:H], b1[:H], b2[:H]],...  1.52 us
    ppermute x1, waiting for transfers between devices, per_device(): got = lax.ppermute(send, 'gy', swap)  1.31 us
    ppermute x1, waiting for transfers between devices, per_device(): return (mask - lax.ppermute(send, 'gy', swap), resist)  1.12 us
  transfers between devices with their start and end apart: 7, of which 4 were waited for; matrix products, arithmetic and copies ran while one was open for 0% of the time, Pallas kernels for 3%

profile of v5, /device:TPU:0, one launch (start us, length us, event | category | flops | bytes accessed | tf_op | source)
XLA Modules:
  0.0 29.6 jit_solution(9182015927042940162)
XLA Ops:
  0.6 0.0 copy-start.9
  0.6 0.9 %convert_element_type.5 = f32[128,128]{1,0:T(8,128)S(1)} convert(s32[128,128]{1,0:T(8,128)} %param.13) | non-fusion elementwise | flops 16384 | bytes 131072 | tf_op jit(solution)/shard_map/convert_element_type | solution.py:307
  1.5 0.0 copy-done.9
  1.5 0.5 %collective-permute-start.1 = (f32[256,128]{1,0:T(8,128)S(1)}, f32[256,128]{1,0:T(8,128)S(1)}, u32[]{:S(2)}, u32[]{:S(2)}) collective-permute-start(f32[256,128]{1,0:T(8,128)S(1)} %pad_maximum_fusion.near_ref), channel_id=1, source_target_pairs={{0,1},{1,3},{2,0},{3,5},{4,2},{5,7},{6,4},{7,9},{8,6},{9,11},{10,8... | collective-permute-start | bytes 393224 | tf_op jit(solution)/shard_map/ppermute | solution.py:314
  2.0 2.6 %collective-permute-start = (f32[256,128]{1,0:T(8,128)S(1)}, f32[256,128]{1,0:T(8,128)S(1)}, u32[]{:S(2)}, u32[]{:S(2)}) collective-permute-start(f32[256,128]{1,0:T(8,128)S(1)} %pad_maximum_fusion.near_ref), channel_id=1, source_target_pairs={{0,2},{1,0},{2,4},{3,1},{4,6},{5,3},{6,8},{7,5},{8,10},{9,7},{10,1... | collective-permute-start | bytes 393224 | tf_op jit(solution)/shard_map/ppermute | solution.py:313
  4.7 0.0 collective-permute-start.3
  4.7 0.0 slice-start
  4.7 2.0 %collective-permute-start.2 = (f32[192,128]{1,0:T(8,128)S(1)}, f32[192,128]{1,0:T(8,128)S(1)}, u32[]{:S(2)}, u32[]{:S(2)}) collective-permute-start(f32[192,128]{1,0:T(8,128)S(1)} %get-tuple-element.31), channel_id=1, source_target_pairs={{0,4},{1,0},{2,6},{3,2},{4,8},{5,1},{6,10},{7,3},{8,12},{9,5},{10,... | collective-permute-start | bytes 294920 | tf_op jit(solution)/shard_map/ppermute | solution.py:315
  6.7 0.0 slice-done
  6.7 0.0 copy-start.6
  6.7 0.0 copy-start.7
  6.7 0.0 copy-start.8
  6.8 0.9 %copy-done.6 = bf16[768,256]{1,0:T(8,128)(2,1)S(1)} copy-done((bf16[768,256]{1,0:T(8,128)(2,1)S(1)}, bf16[768,256]{1,0:T(8,128)(2,1)}, u32[]{:S(2)}) %copy-start.6) | copy-done | bytes 393240
  7.7 0.0 copy-done.7
  7.7 0.0 copy-done.8
  7.7 0.0 copy-start.1
  7.7 0.0 copy-start.2
  7.7 0.0 copy-start.3
  7.8 0.0 copy-start.4
  7.8 0.9 %spectra.1 = (f32[6,128,128]{2,1,0:T(8,128)S(1)}, f32[6,128,128]{2,1,0:T(8,128)S(1)}) custom-call(f32[432,256]{1,0:T(8,128)S(1)} %bitcast.1, bf16[768,256]{1,0:T(8,128)(2,1)S(1)} %copy-done.6, bf16[128,216]{1,0:T(8,128)(2,1)S(1)} %copy-done.8, bf16[128,216]{1,0:T(8,128)(2,1)S(1)} %copy-done.7), custom_call_target="tpu_custom_call" | custom-call | flops 679477248 | bytes 1572864 | tf_op jit(solution)/shard_map/spectra/pallas_call | solution.py:283
  8.7 0.0 copy-start
  8.7 3.7 %collective-permute-done.3.b2_ref = f32[192,128]{1,0:T(8,128)S(1)} collective-permute-done((f32[192,128]{1,0:T(8,128)S(1)}, f32[192,128]{1,0:T(8,128)S(1)}, u32[]{:S(2)}, u32[]{:S(2)}) %collective-permute-start.3) | collective-permute-done | bytes 98336 | tf_op jit(solution)/shard_map/ppermute | solution.py:316
  12.4 0.0 collective-permute-done.2.a2_ref
  12.4 0.0 collective-permute-done.1.b1_ref
  12.4 0.0 collective-permute-done.a1_ref
  12.4 0.0 copy-start.5
  12.5 0.2 collective-permute-start.4
  12.7 1.5 %collective-permute-done.4.mate_ref = f32[640,128]{1,0:T(8,128)S(1)} collective-permute-done((f32[640,128]{1,0:T(8,128)S(1)}, f32[640,128]{1,0:T(8,128)S(1)}, u32[]{:S(2)}, u32[]{:S(2)}) %collective-permute-start.4) | collective-permute-done | bytes 327712 | tf_op jit(solution)/shard_map/ppermute | solution.py:320
  14.2 0.0 copy-done.1
  14.2 0.0 copy-done.2
  14.2 0.0 copy-done.3
  14.2 0.0 copy-done.4
  14.2 0.0 copy-done
  14.2 0.0 copy-done.5
  14.2 7.3 %first_step.1 = (f32[384,256]{1,0:T(8,128)S(1)}, f32[384,128]{1,0:T(8,128)S(1)}, f32[256,128]{1,0:T(8,128)S(1)}) custom-call(f32[256,128]{1,0:T(8,128)S(1)} %pad_maximum_fusion.near_ref, f32[256,128]{1,0:T(8,128)S(1)} %collective-permute-done.a1_ref, f32[256,128]{1,0:T(8,128)S(1)} %collective-permute-done.1.b1_ref, ...), custom_call_target="tpu_custom_call" | custom-call | tf_op jit(solution)/shard_map/first_step/pallas_call | solution.py:325
  21.6 0.2 collective-permute-start.5
  21.8 1.3 %collective-permute-done.5.got_ref = f32[384,128]{1,0:T(8,128)S(1)} collective-permute-done((f32[384,128]{1,0:T(8,128)S(1)}, f32[384,128]{1,0:T(8,128)S(1)}, u32[]{:S(2)}, u32[]{:S(2)}) %collective-permute-start.5) | collective-permute-done | bytes 196640 | tf_op jit(solution)/shard_map/ppermute | solution.py:334
  23.1 4.7 %second_step.1 = (f32[128,128]{1,0:T(8,128)S(1)}, f32[128,128]{1,0:T(8,128)S(1)}, f32[128,128]{1,0:T(8,128)}) custom-call(f32[384,256]{1,0:T(8,128)S(1)} %get-tuple-element.24.rest_ref, f32[384,128]{1,0:T(8,128)S(1)} %collective-permute-done.5.got_ref, f32[256,128]{1,0:T(8,128)S(1)} %get-tuple-element.26.target_ref, ...), custom_call_target="tpu_custom_call" | custom-call | tf_op jit(solution)/shard_map/second_step/pallas_call | solution.py:335
  27.8 0.1 collective-permute-start.6
  27.9 1.1 %collective-permute-done.6 = f32[128,128]{1,0:T(8,128)S(1)} collective-permute-done((f32[128,128]{1,0:T(8,128)S(1)}, f32[128,128]{1,0:T(8,128)S(1)}, u32[]{:S(2)}, u32[]{:S(2)}) %collective-permute-start.6) | collective-permute-done | bytes 65568 | tf_op jit(solution)/shard_map/ppermute | solution.py:344
  29.0 0.6 %sub.3 = f32[128,128]{1,0:T(8,128)} subtract(f32[128,128]{1,0:T(8,128)S(1)} %get-tuple-element.27, f32[128,128]{1,0:T(8,128)S(1)} %collective-permute-done.6) | non-fusion elementwise | flops 16384 | bytes 196608 | tf_op jit(solution)/shard_map/sub | solution.py:344
  (9 shorter events, 0.1 us)
Async XLA Ops:
  0.6 0.9 %copy-start.9 = (f32[128,128]{1,0:T(8,128)S(1)}, f32[128,128]{1,0:T(8,128)}, u32[]{:S(2)}) copy-start(f32[128,128]{1,0:T(8,128)} %param.12) | copy-start | bytes 196612
  1.5 10.9 %collective-permute-start.1 = (f32[256,128]{1,0:T(8,128)S(1)}, f32[256,128]{1,0:T(8,128)S(1)}, u32[]{:S(2)}, u32[]{:S(2)}) collective-permute-start(f32[256,128]{1,0:T(8,128)S(1)} %pad_maximum_fusion.near_ref), channel_id=1, source_target_pairs={{0,1},{1,3},{2,0},{3,5},{4,2},{5,7},{6,4},{7,9},{8,6},{9,11},{10,8... | collective-permute-start | bytes 393224 | tf_op jit(solution)/shard_map/ppermute | solution.py:314
  2.0 10.4 %collective-permute-start = (f32[256,128]{1,0:T(8,128)S(1)}, f32[256,128]{1,0:T(8,128)S(1)}, u32[]{:S(2)}, u32[]{:S(2)}) collective-permute-start(f32[256,128]{1,0:T(8,128)S(1)} %pad_maximum_fusion.near_ref), channel_id=1, source_target_pairs={{0,2},{1,0},{2,4},{3,1},{4,6},{5,3},{6,8},{7,5},{8,10},{9,7},{10,1... | collective-permute-start | bytes 393224 | tf_op jit(solution)/shard_map/ppermute | solution.py:313
  4.7 7.8 %collective-permute-start.3 = (f32[192,128]{1,0:T(8,128)S(1)}, f32[192,128]{1,0:T(8,128)S(1)}, u32[]{:S(2)}, u32[]{:S(2)}) collective-permute-start(f32[192,128]{1,0:T(8,128)S(1)} %get-tuple-element.30), channel_id=1, source_target_pairs={{0,1},{1,5},{2,3},{3,7},{4,0},{5,9},{6,2},{7,11},{8,4},{9,13},{10,... | collective-permute-start | bytes 294920 | tf_op jit(solution)/shard_map/ppermute | solution.py:316
  4.7 2.0 %slice-start = ((f32[6,129,129]{2,1,0:T(8,128)}), f32[6,65,129]{2,1,0:T(8,128)S(1)}, s32[]{:S(2)}) async-start(f32[6,129,129]{2,1,0:T(8,128)} %param.14), calls=%async_computation | async-start | bytes 884736 | tf_op jit(solution)/shard_map/slice | solution.py:277
  4.7 7.7 %collective-permute-start.2 = (f32[192,128]{1,0:T(8,128)S(1)}, f32[192,128]{1,0:T(8,128)S(1)}, u32[]{:S(2)}, u32[]{:S(2)}) collective-permute-start(f32[192,128]{1,0:T(8,128)S(1)} %get-tuple-element.31), channel_id=1, source_target_pairs={{0,4},{1,0},{2,6},{3,2},{4,8},{5,1},{6,10},{7,3},{8,12},{9,5},{10,... | collective-permute-start | bytes 294920 | tf_op jit(solution)/shard_map/ppermute | solution.py:315
  6.7 1.0 %copy-start.6 = (bf16[768,256]{1,0:T(8,128)(2,1)S(1)}, bf16[768,256]{1,0:T(8,128)(2,1)}, u32[]{:S(2)}) copy-start(bf16[768,256]{1,0:T(8,128)(2,1)} %constant.26.clone.right_ref) | copy-start | bytes 1179652
  6.7 1.0 %copy-start.7 = (bf16[128,216]{1,0:T(8,128)(2,1)S(1)}, bf16[128,216]{1,0:T(8,128)(2,1)}, u32[]{:S(2)}) copy-start(bf16[128,216]{1,0:T(8,128)(2,1)} %constant.28.clone.sin_ref) | copy-start | bytes 165892
  6.7 1.0 %copy-start.8 = (bf16[128,216]{1,0:T(8,128)(2,1)S(1)}, bf16[128,216]{1,0:T(8,128)(2,1)}, u32[]{:S(2)}) copy-start(bf16[128,216]{1,0:T(8,128)(2,1)} %constant.27.clone.cos_ref) | copy-start | bytes 165892
  7.7 6.5 %copy-start.1 = (bf16[768,256]{1,0:T(8,128)(2,1)S(1)}, bf16[768,256]{1,0:T(8,128)(2,1)}, u32[]{:S(2)}) copy-start(bf16[768,256]{1,0:T(8,128)(2,1)} %constant.33.clone.refs_4_) | copy-start | bytes 1179652
  7.7 6.5 %copy-start.2 = (bf16[2,384,256]{2,1,0:T(8,128)(2,1)S(1)}, bf16[2,384,256]{2,1,0:T(8,128)(2,1)}, u32[]{:S(2)}) copy-start(bf16[2,384,256]{2,1,0:T(8,128)(2,1)} %constant.31.clone.refs_2_) | copy-start | bytes 1179652
  7.7 6.5 %copy-start.3 = (bf16[768,256]{1,0:T(8,128)(2,1)S(1)}, bf16[768,256]{1,0:T(8,128)(2,1)}, u32[]{:S(2)}) copy-start(bf16[768,256]{1,0:T(8,128)(2,1)} %constant.30.clone.refs_1_) | copy-start | bytes 1179652
  7.8 6.5 %copy-start.4 = (bf16[256,768]{1,0:T(8,128)(2,1)S(1)}, bf16[256,768]{1,0:T(8,128)(2,1)}, u32[]{:S(2)}) copy-start(bf16[256,768]{1,0:T(8,128)(2,1)} %constant.29.clone.refs_0_) | copy-start | bytes 1179652
  8.7 5.5 %copy-start = (bf16[2,768,128]{2,1,0:T(8,128)(2,1)S(1)}, bf16[2,768,128]{2,1,0:T(8,128)(2,1)}, u32[]{:S(2)}) copy-start(bf16[2,768,128]{2,1,0:T(8,128)(2,1)} %constant.34.clone.refs_5_) | copy-start | bytes 1179652
  12.4 1.8 %copy-start.5 = (bf16[128,768]{1,0:T(8,128)(2,1)S(1)}, bf16[128,768]{1,0:T(8,128)(2,1)}, u32[]{:S(2)}) copy-start(bf16[128,768]{1,0:T(8,128)(2,1)} %constant.32.clone.refs_3_) | copy-start | bytes 589828
  12.5 1.7 %collective-permute-start.4 = (f32[640,128]{1,0:T(8,128)S(1)}, f32[640,128]{1,0:T(8,128)S(1)}, u32[]{:S(2)}, u32[]{:S(2)}) collective-permute-start(f32[640,128]{1,0:T(8,128)S(1)} %slice_dynamic-update-slice_fusion), channel_id=1, source_target_pairs={{0,1},{1,0},{2,3},{3,2},{4,5},{5,4},{6,7},{7,6},{8,9},{9,8},{10,11... | collective-permute-start | bytes 983048 | tf_op jit(solution)/shard_map/ppermute | solution.py:320
  21.6 1.5 %collective-permute-start.5 = (f32[384,128]{1,0:T(8,128)S(1)}, f32[384,128]{1,0:T(8,128)S(1)}, u32[]{:S(2)}, u32[]{:S(2)}) collective-permute-start(f32[384,128]{1,0:T(8,128)S(1)} %get-tuple-element.25), channel_id=1, source_target_pairs={{0,1},{1,0},{2,3},{3,2},{4,5},{5,4},{6,7},{7,6},{8,9},{9,8},{10,11... | collective-permute-start | bytes 589832 | tf_op jit(solution)/shard_map/ppermute | solution.py:334
  27.8 1.3 %collective-permute-start.6 = (f32[128,128]{1,0:T(8,128)S(1)}, f32[128,128]{1,0:T(8,128)S(1)}, u32[]{:S(2)}, u32[]{:S(2)}) collective-permute-start(f32[128,128]{1,0:T(8,128)S(1)} %get-tuple-element.28), channel_id=1, source_target_pairs={{0,1},{1,0},{2,3},{3,2},{4,5},{5,4},{6,7},{7,6},{8,9},{9,8},{10,11... | collective-permute-start | bytes 196616 | tf_op jit(solution)/shard_map/ppermute | solution.py:344

commit v6 on v5

--- a/solution.py
+++ b/solution.py
@@ -85,9 +85,10 @@
 
 
 def pipeline(count, *stages):
-    for step in range(count + 2 * (len(stages) - 1)):
+    lag = 1 if count <= 12 else 2
+    for step in range(count + lag * (len(stages) - 1)):
         for place, stage in enumerate(stages):
-            item = step - 2 * place
+            item = step - lag * place
             if 0 <= item < count:
                 stage(item)
 

time: 29.8 us -> 29.9 us (level)
  no operation moved by 1% of the time
where the time goes in v6:
time: 29.9 us; the launch traced here: 29.8 us
  Pallas kernels  13 us (43%)
  waiting for transfers between devices  7.68 us (26%)
  starting transfers between devices  5.65 us (19%)
  other arithmetic  1.55 us (5%)
  local copies, waits for them, and re-layouts  1.07 us (4%)
  between operations  0.81 us (3%)
    pallas_call x1, Pallas kernels, per_device(): pl.pallas_call(functools.partial(first_kernel, tiles), out_shape=(shape(3...  7.44 us
    pallas_call x1, Pallas kernels, per_device(): pl.pallas_call(functools.partial(second_kernel, tiles), out_shape=(shape(...  4.66 us
    ppermute x1, waiting for transfers between devices, per_device(): lax.ppermute(down, both, ring(-2))  3.72 us
    ppermute x1, starting transfers between devices, per_device(): lax.ppermute(near, both, ring(1))  2.58 us
    ppermute x1, starting transfers between devices, per_device(): lax.ppermute(up, both, ring(2))  2.03 us
    ppermute x1, waiting for transfers between devices, per_device(): lax.ppermute(jnp.concatenate([a2[:H], a1[:H], near[:H], b1[:H], b2[:H]],...  1.52 us
    ppermute x1, waiting for transfers between devices, per_device(): got = lax.ppermute(send, 'gy', swap)  1.31 us
    ppermute x1, waiting for transfers between devices, per_device(): return (mask - lax.ppermute(send, 'gy', swap), resist)  1.11 us
  transfers between devices with their start and end apart: 7, of which 4 were waited for; matrix products, arithmetic and copies ran while one was open for 0% of the time, Pallas kernels for 3%

profile of v6, /device:TPU:0, one launch (start us, length us, event | category | flops | bytes accessed | tf_op | source)
XLA Modules:
  0.0 29.8 jit_solution(10748430568574760218)
XLA Ops:
  0.6 0.0 copy-start.9
  0.6 0.9 %convert_element_type.5 = f32[128,128]{1,0:T(8,128)S(1)} convert(s32[128,128]{1,0:T(8,128)} %param.13) | non-fusion elementwise | flops 16384 | bytes 131072 | tf_op jit(solution)/shard_map/convert_element_type | solution.py:308
  1.5 0.0 copy-done.9
  1.5 0.5 %collective-permute-start.1 = (f32[256,128]{1,0:T(8,128)S(1)}, f32[256,128]{1,0:T(8,128)S(1)}, u32[]{:S(2)}, u32[]{:S(2)}) collective-permute-start(f32[256,128]{1,0:T(8,128)S(1)} %pad_maximum_fusion.near_ref), channel_id=1, source_target_pairs={{0,1},{1,3},{2,0},{3,5},{4,2},{5,7},{6,4},{7,9},{8,6},{9,11},{10,8... | collective-permute-start | bytes 393224 | tf_op jit(solution)/shard_map/ppermute | solution.py:315
  2.0 2.6 %collective-permute-start = (f32[256,128]{1,0:T(8,128)S(1)}, f32[256,128]{1,0:T(8,128)S(1)}, u32[]{:S(2)}, u32[]{:S(2)}) collective-permute-start(f32[256,128]{1,0:T(8,128)S(1)} %pad_maximum_fusion.near_ref), channel_id=1, source_target_pairs={{0,2},{1,0},{2,4},{3,1},{4,6},{5,3},{6,8},{7,5},{8,10},{9,7},{10,1... | collective-permute-start | bytes 393224 | tf_op jit(solution)/shard_map/ppermute | solution.py:314
  4.7 0.0 collective-permute-start.3
  4.7 0.0 slice-start
  4.7 2.0 %collective-permute-start.2 = (f32[192,128]{1,0:T(8,128)S(1)}, f32[192,128]{1,0:T(8,128)S(1)}, u32[]{:S(2)}, u32[]{:S(2)}) collective-permute-start(f32[192,128]{1,0:T(8,128)S(1)} %get-tuple-element.31), channel_id=1, source_target_pairs={{0,4},{1,0},{2,6},{3,2},{4,8},{5,1},{6,10},{7,3},{8,12},{9,5},{10,... | collective-permute-start | bytes 294920 | tf_op jit(solution)/shard_map/ppermute | solution.py:316
  6.7 0.0 slice-done
  6.7 0.0 copy-start.6
  6.7 0.0 copy-start.7
  6.7 0.0 copy-start.8
  6.8 0.9 %copy-done.6 = bf16[768,256]{1,0:T(8,128)(2,1)S(1)} copy-done((bf16[768,256]{1,0:T(8,128)(2,1)S(1)}, bf16[768,256]{1,0:T(8,128)(2,1)}, u32[]{:S(2)}) %copy-start.6) | copy-done | bytes 393240
  7.7 0.0 copy-done.7
  7.7 0.0 copy-done.8
  7.7 0.0 copy-start.1
  7.7 0.0 copy-start.2
  7.7 0.0 copy-start.3
  7.8 0.0 copy-start.4
  7.8 0.9 %spectra.1 = (f32[6,128,128]{2,1,0:T(8,128)S(1)}, f32[6,128,128]{2,1,0:T(8,128)S(1)}) custom-call(f32[432,256]{1,0:T(8,128)S(1)} %bitcast.1, bf16[768,256]{1,0:T(8,128)(2,1)S(1)} %copy-done.6, bf16[128,216]{1,0:T(8,128)(2,1)S(1)} %copy-done.8, bf16[128,216]{1,0:T(8,128)(2,1)S(1)} %copy-done.7), custom_call_target="tpu_custom_call" | custom-call | flops 679477248 | bytes 1572864 | tf_op jit(solution)/shard_map/spectra/pallas_call | solution.py:284
  8.7 0.0 copy-start
  8.7 3.7 %collective-permute-done.3.b2_ref = f32[192,128]{1,0:T(8,128)S(1)} collective-permute-done((f32[192,128]{1,0:T(8,128)S(1)}, f32[192,128]{1,0:T(8,128)S(1)}, u32[]{:S(2)}, u32[]{:S(2)}) %collective-permute-start.3) | collective-permute-done | bytes 98336 | tf_op jit(solution)/shard_map/ppermute | solution.py:317
  12.4 0.0 collective-permute-done.2.a2_ref
  12.4 0.0 collective-permute-done.1.b1_ref
  12.4 0.0 collective-permute-done.a1_ref
  12.4 0.0 copy-start.5
  12.5 0.2 collective-permute-start.4
  12.7 1.5 %collective-permute-done.4.mate_ref = f32[640,128]{1,0:T(8,128)S(1)} collective-permute-done((f32[640,128]{1,0:T(8,128)S(1)}, f32[640,128]{1,0:T(8,128)S(1)}, u32[]{:S(2)}, u32[]{:S(2)}) %collective-permute-start.4) | collective-permute-done | bytes 327712 | tf_op jit(solution)/shard_map/ppermute | solution.py:321
  14.2 0.0 copy-done.1
  14.2 0.0 copy-done.2
  14.2 0.0 copy-done.3
  14.2 0.0 copy-done.4
  14.2 0.0 copy-done
  14.2 0.0 copy-done.5
  14.2 7.4 %first_step.1 = (f32[384,256]{1,0:T(8,128)S(1)}, f32[384,128]{1,0:T(8,128)S(1)}, f32[256,128]{1,0:T(8,128)S(1)}) custom-call(f32[256,128]{1,0:T(8,128)S(1)} %pad_maximum_fusion.near_ref, f32[256,128]{1,0:T(8,128)S(1)} %collective-permute-done.a1_ref, f32[256,128]{1,0:T(8,128)S(1)} %collective-permute-done.1.b1_ref, ...), custom_call_target="tpu_custom_call" | custom-call | tf_op jit(solution)/shard_map/first_step/pallas_call | solution.py:326
  21.7 0.2 collective-permute-start.5
  21.9 1.3 %collective-permute-done.5.got_ref = f32[384,128]{1,0:T(8,128)S(1)} collective-permute-done((f32[384,128]{1,0:T(8,128)S(1)}, f32[384,128]{1,0:T(8,128)S(1)}, u32[]{:S(2)}, u32[]{:S(2)}) %collective-permute-start.5) | collective-permute-done | bytes 196640 | tf_op jit(solution)/shard_map/ppermute | solution.py:335
  23.2 4.7 %second_step.1 = (f32[128,128]{1,0:T(8,128)S(1)}, f32[128,128]{1,0:T(8,128)S(1)}, f32[128,128]{1,0:T(8,128)}) custom-call(f32[384,256]{1,0:T(8,128)S(1)} %get-tuple-element.24.rest_ref, f32[384,128]{1,0:T(8,128)S(1)} %collective-permute-done.5.got_ref, f32[256,128]{1,0:T(8,128)S(1)} %get-tuple-element.26.target_ref, ...), custom_call_target="tpu_custom_call" | custom-call | tf_op jit(solution)/shard_map/second_step/pallas_call | solution.py:336
  27.9 0.1 collective-permute-start.6
  28.0 1.1 %collective-permute-done.6 = f32[128,128]{1,0:T(8,128)S(1)} collective-permute-done((f32[128,128]{1,0:T(8,128)S(1)}, f32[128,128]{1,0:T(8,128)S(1)}, u32[]{:S(2)}, u32[]{:S(2)}) %collective-permute-start.6) | collective-permute-done | bytes 65568 | tf_op jit(solution)/shard_map/ppermute | solution.py:345
  29.1 0.6 %sub.3 = f32[128,128]{1,0:T(8,128)} subtract(f32[128,128]{1,0:T(8,128)S(1)} %get-tuple-element.27, f32[128,128]{1,0:T(8,128)S(1)} %collective-permute-done.6) | non-fusion elementwise | flops 16384 | bytes 196608 | tf_op jit(solution)/shard_map/sub | solution.py:345
  (9 shorter events, 0.1 us)
Async XLA Ops:
  0.6 0.9 %copy-start.9 = (f32[128,128]{1,0:T(8,128)S(1)}, f32[128,128]{1,0:T(8,128)}, u32[]{:S(2)}) copy-start(f32[128,128]{1,0:T(8,128)} %param.12) | copy-start | bytes 196612
  1.5 10.9 %collective-permute-start.1 = (f32[256,128]{1,0:T(8,128)S(1)}, f32[256,128]{1,0:T(8,128)S(1)}, u32[]{:S(2)}, u32[]{:S(2)}) collective-permute-start(f32[256,128]{1,0:T(8,128)S(1)} %pad_maximum_fusion.near_ref), channel_id=1, source_target_pairs={{0,1},{1,3},{2,0},{3,5},{4,2},{5,7},{6,4},{7,9},{8,6},{9,11},{10,8... | collective-permute-start | bytes 393224 | tf_op jit(solution)/shard_map/ppermute | solution.py:315
  2.0 10.4 %collective-permute-start = (f32[256,128]{1,0:T(8,128)S(1)}, f32[256,128]{1,0:T(8,128)S(1)}, u32[]{:S(2)}, u32[]{:S(2)}) collective-permute-start(f32[256,128]{1,0:T(8,128)S(1)} %pad_maximum_fusion.near_ref), channel_id=1, source_target_pairs={{0,2},{1,0},{2,4},{3,1},{4,6},{5,3},{6,8},{7,5},{8,10},{9,7},{10,1... | collective-permute-start | bytes 393224 | tf_op jit(solution)/shard_map/ppermute | solution.py:314
  4.7 7.8 %collective-permute-start.3 = (f32[192,128]{1,0:T(8,128)S(1)}, f32[192,128]{1,0:T(8,128)S(1)}, u32[]{:S(2)}, u32[]{:S(2)}) collective-permute-start(f32[192,128]{1,0:T(8,128)S(1)} %get-tuple-element.30), channel_id=1, source_target_pairs={{0,1},{1,5},{2,3},{3,7},{4,0},{5,9},{6,2},{7,11},{8,4},{9,13},{10,... | collective-permute-start | bytes 294920 | tf_op jit(solution)/shard_map/ppermute | solution.py:317
  4.7 2.0 %slice-start = ((f32[6,129,129]{2,1,0:T(8,128)}), f32[6,65,129]{2,1,0:T(8,128)S(1)}, s32[]{:S(2)}) async-start(f32[6,129,129]{2,1,0:T(8,128)} %param.14), calls=%async_computation | async-start | bytes 884736 | tf_op jit(solution)/shard_map/slice | solution.py:278
  4.7 7.7 %collective-permute-start.2 = (f32[192,128]{1,0:T(8,128)S(1)}, f32[192,128]{1,0:T(8,128)S(1)}, u32[]{:S(2)}, u32[]{:S(2)}) collective-permute-start(f32[192,128]{1,0:T(8,128)S(1)} %get-tuple-element.31), channel_id=1, source_target_pairs={{0,4},{1,0},{2,6},{3,2},{4,8},{5,1},{6,10},{7,3},{8,12},{9,5},{10,... | collective-permute-start | bytes 294920 | tf_op jit(solution)/shard_map/ppermute | solution.py:316
  6.7 1.0 %copy-start.6 = (bf16[768,256]{1,0:T(8,128)(2,1)S(1)}, bf16[768,256]{1,0:T(8,128)(2,1)}, u32[]{:S(2)}) copy-start(bf16[768,256]{1,0:T(8,128)(2,1)} %constant.26.clone.right_ref) | copy-start | bytes 1179652
  6.7 1.0 %copy-start.7 = (bf16[128,216]{1,0:T(8,128)(2,1)S(1)}, bf16[128,216]{1,0:T(8,128)(2,1)}, u32[]{:S(2)}) copy-start(bf16[128,216]{1,0:T(8,128)(2,1)} %constant.28.clone.sin_ref) | copy-start | bytes 165892
  6.7 1.0 %copy-start.8 = (bf16[128,216]{1,0:T(8,128)(2,1)S(1)}, bf16[128,216]{1,0:T(8,128)(2,1)}, u32[]{:S(2)}) copy-start(bf16[128,216]{1,0:T(8,128)(2,1)} %constant.27.clone.cos_ref) | copy-start | bytes 165892
  7.7 6.5 %copy-start.1 = (bf16[768,256]{1,0:T(8,128)(2,1)S(1)}, bf16[768,256]{1,0:T(8,128)(2,1)}, u32[]{:S(2)}) copy-start(bf16[768,256]{1,0:T(8,128)(2,1)} %constant.33.clone.refs_4_) | copy-start | bytes 1179652
  7.7 6.5 %copy-start.2 = (bf16[2,384,256]{2,1,0:T(8,128)(2,1)S(1)}, bf16[2,384,256]{2,1,0:T(8,128)(2,1)}, u32[]{:S(2)}) copy-start(bf16[2,384,256]{2,1,0:T(8,128)(2,1)} %constant.31.clone.refs_2_) | copy-start | bytes 1179652
  7.7 6.5 %copy-start.3 = (bf16[768,256]{1,0:T(8,128)(2,1)S(1)}, bf16[768,256]{1,0:T(8,128)(2,1)}, u32[]{:S(2)}) copy-start(bf16[768,256]{1,0:T(8,128)(2,1)} %constant.30.clone.refs_1_) | copy-start | bytes 1179652
  7.8 6.5 %copy-start.4 = (bf16[256,768]{1,0:T(8,128)(2,1)S(1)}, bf16[256,768]{1,0:T(8,128)(2,1)}, u32[]{:S(2)}) copy-start(bf16[256,768]{1,0:T(8,128)(2,1)} %constant.29.clone.refs_0_) | copy-start | bytes 1179652
  8.7 5.5 %copy-start = (bf16[2,768,128]{2,1,0:T(8,128)(2,1)S(1)}, bf16[2,768,128]{2,1,0:T(8,128)(2,1)}, u32[]{:S(2)}) copy-start(bf16[2,768,128]{2,1,0:T(8,128)(2,1)} %constant.34.clone.refs_5_) | copy-start | bytes 1179652
  12.4 1.8 %copy-start.5 = (bf16[128,768]{1,0:T(8,128)(2,1)S(1)}, bf16[128,768]{1,0:T(8,128)(2,1)}, u32[]{:S(2)}) copy-start(bf16[128,768]{1,0:T(8,128)(2,1)} %constant.32.clone.refs_3_) | copy-start | bytes 589828
  12.5 1.7 %collective-permute-start.4 = (f32[640,128]{1,0:T(8,128)S(1)}, f32[640,128]{1,0:T(8,128)S(1)}, u32[]{:S(2)}, u32[]{:S(2)}) collective-permute-start(f32[640,128]{1,0:T(8,128)S(1)} %slice_dynamic-update-slice_fusion), channel_id=1, source_target_pairs={{0,1},{1,0},{2,3},{3,2},{4,5},{5,4},{6,7},{7,6},{8,9},{9,8},{10,11... | collective-permute-start | bytes 983048 | tf_op jit(solution)/shard_map/ppermute | solution.py:321
  21.7 1.5 %collective-permute-start.5 = (f32[384,128]{1,0:T(8,128)S(1)}, f32[384,128]{1,0:T(8,128)S(1)}, u32[]{:S(2)}, u32[]{:S(2)}) collective-permute-start(f32[384,128]{1,0:T(8,128)S(1)} %get-tuple-element.25), channel_id=1, source_target_pairs={{0,1},{1,0},{2,3},{3,2},{4,5},{5,4},{6,7},{7,6},{8,9},{9,8},{10,11... | collective-permute-start | bytes 589832 | tf_op jit(solution)/shard_map/ppermute | solution.py:335
  27.9 1.3 %collective-permute-start.6 = (f32[128,128]{1,0:T(8,128)S(1)}, f32[128,128]{1,0:T(8,128)S(1)}, u32[]{:S(2)}, u32[]{:S(2)}) collective-permute-start(f32[128,128]{1,0:T(8,128)S(1)} %get-tuple-element.28), channel_id=1, source_target_pairs={{0,1},{1,0},{2,3},{3,2},{4,5},{5,4},{6,7},{7,6},{8,9},{9,8},{10,11... | collective-permute-start | bytes 196616 | tf_op jit(solution)/shard_map/ppermute | solution.py:345
